TPU v7x, 512 devices: a whole 4x8x8 slice. The times are simulated.
512 devices in a mesh: dop: 16 (over z, core), rng: 32 (over x, y).
Axes of the slice: x: 4, y: 8, z: 8, core: 2. Of those that a mesh axis runs over, the one named last changes fastest.
Arguments:
- cube: bfloat16 [2, 64, 128, 16384], P(None, None, 'dop', 'rng'), may hold values from -200 to 200
- train_blocks: int32 [128, 128], P('dop', 'rng'), may hold values 0 or 1
- guard_blocks: int32 [128], P('rng'), may hold values 0 or 1
- prior_factor: float32 [128, 256, 256], P('dop', 'rng'), may hold values from -1638400 to 1638400, as said below
- steering: float32 [128, 256], P('dop'), may hold values from -6 to 6
Outputs:
- filtered: float32 [2, 128, 16384], P(None, 'dop', 'rng')
- factor: float32 [128, 256, 256], P('dop', 'rng')
Inputs may be any that keep to these rules, and one draw needn't show every extreme that they name: `prior_factor`: upper triangular with a positive diagonal.
All inputs are finite; a program needn't handle non-finite values. No bound on the sum of `train_blocks` or of `guard_blocks` on one device may be relied on, other than what follows from the above.
Results may differ from a plain program's by a relative error of at most 0.0041.
Values may be sent and summed in bfloat16 or wider, within the bound.
A program may use at most 64 MiB of HBM per device.

v0:
```python
import math

import jax
import jax.numpy as jnp
from jax import lax
from jax.sharding import PartitionSpec as P

BLOCK = 128


forgetting = 0.98


def from_behind(block, axis, distance):
    devices = range(lax.axis_size(axis))
    route = [((i - distance) % len(devices), i) for i in devices]
    return lax.ppermute(block, axis, route)


def dft_table(pulses):
    index = jnp.arange(pulses, dtype=jnp.int32)
    product = index[:, None] * index[None, :] % pulses
    angle = product.astype(jnp.float32) * (2.0 * math.pi / pulses)
    cosine = jnp.cos(angle)
    sine = jnp.sin(angle)
    top = jnp.stack([cosine, -sine], axis=1)
    bottom = jnp.stack([sine, cosine], axis=1)
    return jnp.stack([top, bottom], axis=0)


def spectra(pulse_block, table):
    out = jnp.einsum(
        "scpg,sptk->tckg", pulse_block.astype(jnp.float32), table, precision=lax.Precision.HIGHEST
    )
    return out.astype(jnp.bfloat16)


def shards(cube, train_blocks, guard_blocks, prior_factor, steering):
    table = dft_table(cube.shape[2] * lax.axis_size("dop"))
    pulse_block = lax.all_to_all(cube, "dop", split_axis=3, concat_axis=2, tiled=True)
    spectrum = lax.all_to_all(
        spectra(pulse_block, table), "dop", split_axis=2, concat_axis=3, tiled=True
    )
    neighbor = from_behind(spectrum[:, :, 0:1, :], "dop", -1)
    following = jnp.concatenate([spectrum[:, :, 1:, :], neighbor], axis=2)
    vectors = jnp.concatenate([spectrum[0], following[0], spectrum[1], following[1]], axis=0)
    usable = train_blocks * guard_blocks[None, :]
    gate_mask = jnp.repeat(usable, BLOCK, axis=1).astype(jnp.bfloat16)
    masked = vectors * gate_mask[None, :, :]
    gram = jnp.einsum("dkg,ekg->kde", masked, masked, preferred_element_type=jnp.float32)
    half = vectors.shape[0] // 2
    real_part = gram[:, :half, :half] + gram[:, half:, half:]
    cross = gram[:, half:, :half] - gram[:, :half, half:]
    prior_gram = forgetting * jnp.einsum(
        "krd,kre->kde", prior_factor, prior_factor, precision=lax.Precision.HIGHEST
    )
    top = jnp.concatenate([real_part, -cross], axis=2)
    bottom = jnp.concatenate([cross, real_part], axis=2)
    local = jnp.concatenate([top, bottom], axis=1) + prior_gram
    covariance = lax.psum(local, "rng")
    lower = jnp.linalg.cholesky(covariance)
    first = lax.linalg.triangular_solve(lower, steering[:, :, None], left_side=True, lower=True)
    second = lax.linalg.triangular_solve(lower, first, left_side=True, lower=True, transpose_a=True)
    weight = second[:, :, 0] / jnp.sum(first[:, :, 0] * first[:, :, 0], axis=1, keepdims=True)
    rotated = jnp.concatenate([-weight[:, half:], weight[:, :half]], axis=1)
    stacked = jnp.stack([weight, rotated]).astype(jnp.bfloat16)
    filtered = jnp.einsum("skd,dkg->skg", stacked, vectors, preferred_element_type=jnp.float32)
    rows = prior_factor.shape[1]
    start = lax.axis_index("rng") * rows
    factor = lax.dynamic_slice_in_dim(jnp.swapaxes(lower, 1, 2), start, rows, axis=1)
    return (filtered, factor)


def solution(mesh):
    return jax.shard_map(
        shards,
        mesh=mesh,
        in_specs=(
            P(None, None, "dop", "rng"),
            P("dop", "rng"),
            P("rng"),
            P("dop", "rng", None),
            P("dop", None),
        ),
        out_specs=(P(None, "dop", "rng"), P("dop", "rng", None)),
        check_vma=False,
    )
```

profile of v0, /device:TPU:1, one launch (start us, length us, event | category | flops | bytes accessed | tf_op | source)
XLA Modules:
  0.0 738.9 jit_solution(6532343640095411719)
XLA Ops:
  7.2 4.0 copy.72
  11.2 2.2 reshape.203
  13.4 11.8 %all-to-all-start = ((bf16[16,2,16384]{2,1,0:T(2,128)(2,1)}), bf16[16,2,16384]{2,1,0:T(2,128)(2,1)S(1)}, u32[]{:S(2)}, u32[]{:S(2)}) async-start(bf16[16,2,16384]{2,1,0:T(2,128)(2,1)} %reshape.203), calls=%async_computation | async-start | bytes 2097152 | tf_op jit(solution)/shard_map/all_to_all | solution.py:40
  25.8 27.4 %all-to-all-done = bf16[16,2,16384]{2,1,0:T(2,128)(2,1)S(1)} async-done(((bf16[16,2,16384]{2,1,0:T(2,128)(2,1)}), bf16[16,2,16384]{2,1,0:T(2,128)(2,1)S(1)}, u32[]{:S(2)}, u32[]{:S(2)}) %all-to-all-start) | async-done | bytes 1048608 | tf_op jit(solution)/shard_map/all_to_all | solution.py:40
  54.6 1.9 copy.74
  56.5 2.9 copy.75
  60.4 3.0 copy.76
  63.4 2.2 reshape.205
  65.6 3.5 all-to-all-start.1
  69.6 27.5 %all-to-all-done.1 = bf16[16,2,16384]{2,1,0:T(2,128)(2,1)S(1)} async-done(((bf16[16,2,16384]{2,1,0:T(2,128)(2,1)}), bf16[16,2,16384]{2,1,0:T(2,128)(2,1)S(1)}, u32[]{:S(2)}, u32[]{:S(2)}) %all-to-all-start.1) | async-done | bytes 1048608 | tf_op jit(solution)/shard_map/all_to_all | solution.py:41
  102.2 3.1 fusion.42
  112.3 3.3 maximum_add_fusion
  116.3 159.7 %all-reduce.3.cloned.1.call-done = f32[8,256,256]{1,2,0:T(8,128)} async-done(((f32[8,256,256]{1,2,0:T(8,128)}), f32[8,256,256]{1,2,0:T(8,128)}) %all-reduce.3.cloned.1.call-update) | async-done | bytes 2097168 | tf_op jit(solution)/shard_map/psum | solution.py:60
  276.0 3.1 copy.86
  279.1 1.9 fusion
  282.3 93.8 %custom-call.18 = f32[8,128,128]{2,1,0:T(8,128)S(1)} custom-call(f32[8,128,128]{2,1,0:T(8,128)S(1)} %cholesky.122), custom_call_target="Cholesky" | custom-call | tf_op jit(solution)/shard_map/jit(cholesky)/cholesky | solution.py:61
  376.4 79.4 %custom-call.19 = f32[8,1,128,128]{2,3,1,0:T(8,128)} custom-call(f32[8,1,128,128]{3,2,1,0:T(8,128)S(1)} %select_bitcast_fusion), custom_call_target="InvertDiagBlocksLowerTriangular" | custom-call | tf_op jit(solution)/shard_map/jit(cholesky)/cholesky | solution.py:61
  457.7 3.1 convolution_subtract_fusion
  460.7 94.6 %custom-call.20 = f32[8,128,128]{2,1,0:T(8,128)S(1)} custom-call(f32[8,128,128]{2,1,0:T(8,128)} %convolution_subtract_fusion), custom_call_target="Cholesky" | custom-call | tf_op jit(solution)/shard_map/jit(cholesky)/cholesky | solution.py:61
  556.7 3.4 broadcast_select_fusion
  560.2 5.8 while.1
  560.8 2.3 bitcast_dynamic-update-slice_fusion.2
  563.8 2.3 bitcast_dynamic-update-slice_fusion.2
  566.1 158.3 %custom-call.21 = f32[8,2,128,128]{2,3,1,0:T(8,128)S(1)} custom-call(f32[8,2,128,128]{3,2,1,0:T(8,128)} %bitcast.155), custom_call_target="InvertDiagBlocksLowerTriangular" | custom-call | tf_op jit(solution)/shard_map/triangular_solve | solution.py:63
  (99 shorter events, 29.7 us)
Async XLA Ops:
  7.2 105.1 %copy-start = (f32[8,8,256]{2,1,0:T(8,128)S(1)}, f32[8,8,256]{2,1,0:T(8,128)}, u32[]{:S(2)}) copy-start(f32[8,8,256]{2,1,0:T(8,128)} %param.8) | copy-start | bytes 196612
  13.4 39.8 %all-to-all-start = ((bf16[16,2,16384]{2,1,0:T(2,128)(2,1)}), bf16[16,2,16384]{2,1,0:T(2,128)(2,1)S(1)}, u32[]{:S(2)}, u32[]{:S(2)}) async-start(bf16[16,2,16384]{2,1,0:T(2,128)(2,1)} %reshape.203), calls=%async_computation | async-start | bytes 2097152 | tf_op jit(solution)/shard_map/all_to_all | solution.py:40
  63.3 6.1 copy-start.16
  63.4 6.1 copy-start.17
  65.6 31.4 %all-to-all-start.1 = ((bf16[16,2,16384]{2,1,0:T(2,128)(2,1)}), bf16[16,2,16384]{2,1,0:T(2,128)(2,1)S(1)}, u32[]{:S(2)}, u32[]{:S(2)}) async-start(bf16[16,2,16384]{2,1,0:T(2,128)(2,1)} %reshape.205), calls=%async_computation.1 | async-start | bytes 2097152 | tf_op jit(solution)/shard_map/all_to_all | solution.py:41
  69.2 206.9 %all-reduce.3.cloned.1.call-start = ((), (), s32[]{:S(2)}) async-start(), calls=%async_computation.2 | async-start | bytes 4194304 | tf_op jit(solution)/shard_map/psum | solution.py:60
  100.6 1.3 copy-start.3
  102.1 6.9 collective-permute-start
  102.2 3.2 copy-start.4
  108.6 1.9 copy-start.7
  109.1 3.0 copy-start.9
  110.5 1.5 copy-start.11
  110.5 1.5 copy-start.13
  115.5 0.7 copy-start.15
  276.0 3.1 copy-start.1
  281.0 1.3 copy-start.5
  555.4 1.3 copy-start.2
  724.3 4.9 copy-start.8
  724.3 4.9 copy-start.10
  724.4 4.9 copy-start.12
  724.4 4.9 copy-start.14
  729.2 1.6 copy-start.6
Sparse Core Ops, SparseCore 0:
  115.7 160.3 all-reduce.2
where the time goes:
time: 742 us; the launch traced here: 739 us
  other arithmetic  434 us (58%)
  waiting for transfers between devices  215 us (29%)
  local copies, waits for them, and re-layouts  44.3 us (6%)
  starting transfers between devices  15.6 us (2%)
  matrix products  15.5 us (2%)
  between operations  14.5 us (2%)
    another operation x10, other arithmetic, shards(): lower = jnp.linalg.cholesky(covariance)  268 us
    another operation x5, other arithmetic, shards(): lax.linalg.triangular_solve(lower, first, left_side=True, lower=True, tra...  162 us
    psum x1, waiting for transfers between devices, shards(): covariance = lax.psum(local, 'rng')  160 us
    all_to_all x1, waiting for transfers between devices, shards(): lax.all_to_all(spectra(pulse_block, table), 'dop', split_axis=2, concat_a...  27.5 us
    all_to_all x1, waiting for transfers between devices, shards(): lax.all_to_all(cube, 'dop', split_axis=3, concat_axis=2, tiled=True)  27.4 us
    unnamed x45, local copies, waits for them, and re-layouts  19.4 us
  transfers between devices with their start and end apart: 4, of which 3 were waited for; matrix products, arithmetic and copies ran while one was open for 1% of the time, Pallas kernels for 0%

commit v1 on v0

--- a/solution.py
+++ b/solution.py
@@ -3,10 +3,14 @@
 import jax
 import jax.numpy as jnp
 from jax import lax
+from jax.experimental import pallas as pl
+from jax.experimental.pallas import tpu as pltpu
 from jax.sharding import PartitionSpec as P
 
 BLOCK = 128
-
+BINS = 8
+LANES = 128
+PANEL = 8
 
 forgetting = 0.98
 
@@ -35,7 +39,120 @@
     return out.astype(jnp.bfloat16)
 
 
+def lane(x, index):
+    where = jnp.full((BINS, LANES), index, jnp.int32)
+    return jnp.take_along_axis(x, where, axis=1, mode="promise_in_bounds")
+
+
+def factor_kernel(cov_ref, steer_ref, out_ref, weight_ref, left, right):
+    halves = (left, right)
+    at = lax.broadcasted_iota(jnp.int32, (BINS, LANES), 1)
+    for h in range(2):
+        halves[h][...] = cov_ref[:, h * LANES : (h + 1) * LANES]
+
+    def rows(j):
+        return pl.ds(pl.multiple_of(j * BINS, BINS), BINS)
+
+    def panel(h, p, carry):
+        s, q, vv = carry
+        o = p * PANEL
+        base = h * LANES + o
+        pair = [[halves[c][rows(base + i), :] for c in range(2)] for i in range(PANEL)]
+        final = []
+        for j in range(PANEL):
+            own = at == o + j
+            pivot = lane(pair[j][h], o + j)
+            inv = lax.rsqrt(pivot)
+            inv2 = inv * inv
+            source = list(pair[j])
+            source[h] = jnp.where(own, 1.0, source[h])
+            for i in range(j + 1, PANEL):
+                m = lane(pair[j][h], o + i) * inv2
+                target = list(pair[i])
+                target[h] = jnp.where(own, 0.0, target[h])
+                pair[i] = [target[c] - m * source[c] for c in range(2)]
+            row = [source[c] * inv for c in range(2)]
+            v = lane(s[h], o + j) * inv
+            s = [s[c] - v * row[c] for c in range(2)]
+            below = [row[0], jnp.zeros_like(row[1])] if h else [row[0], jnp.zeros_like(row[1])]
+            below[h] = jnp.where(at <= o + j, row[h], 0.0)
+            q = [q[c] + v * below[c] for c in range(2)]
+            vv = vv + v * v
+            shown = list(row)
+            if h:
+                shown[0] = jnp.zeros_like(row[0])
+            shown[h] = jnp.where(own, pivot * inv, jnp.where(at > o + j, row[h], 0.0))
+            for c in range(2):
+                halves[c][rows(base + j), :] = row[c]
+                out_ref[rows(base + j), c * LANES : (c + 1) * LANES] = shown[c]
+            row[h] = jnp.where((at > o + j) & (at < o + PANEL), 0.0, row[h])
+            final.append(row)
+        inside = (at >= o) & (at < o + PANEL)
+
+        def group(g, _):
+            for i in range(PANEL):
+                index = g * PANEL + i
+                place = rows(h * LANES + index)
+                target = [halves[c][place, :] for c in range(2)]
+                target[h] = jnp.where(inside, 0.0, target[h])
+                for k in range(PANEL):
+                    m = lane(final[k][h], index)
+                    target = [target[c] - m * final[k][c] for c in range(2)]
+                for c in range(2):
+                    halves[c][place, :] = target[c]
+            return 0
+
+        lax.fori_loop(p + 1, LANES // PANEL, group, 0)
+        return s, q, vv
+
+    zero = jnp.zeros((BINS, LANES), jnp.float32)
+    s = [steer_ref[:, c * LANES : (c + 1) * LANES] for c in range(2)]
+    carry = (s, [zero, zero], zero)
+    carry = lax.fori_loop(0, LANES // PANEL, lambda p, c: panel(0, p, c), carry)
+
+    row_id = lax.broadcasted_iota(jnp.int32, (LANES, LANES), 0)
+    col_id = lax.broadcasted_iota(jnp.int32, (LANES, LANES), 1)
+    for b in range(BINS):
+        top = pl.ds(b, LANES, stride=BINS)
+        bottom = pl.ds(LANES * BINS + b, LANES, stride=BINS)
+        upper = right[top, :]
+        inverse = jnp.where(col_id <= row_id, left[top, :], 0.0)
+        across = upper.T
+        left[bottom, :] = -jnp.dot(
+            across, inverse, precision=lax.Precision.HIGHEST, preferred_element_type=jnp.float32
+        )
+        right[bottom, :] = right[bottom, :] - jnp.dot(
+            across, upper, precision=lax.Precision.HIGHEST, preferred_element_type=jnp.float32
+        )
+
+    s, q, vv = lax.fori_loop(0, LANES // PANEL, lambda p, c: panel(1, p, c), carry)
+    for c in range(2):
+        weight_ref[:, c * LANES : (c + 1) * LANES] = q[c] / vv
+
+
+def factorize(covariance, steering):
+    n = covariance.shape[0]
+    flat = covariance.reshape(n * BINS, n)
+    factor, weight = pl.pallas_call(
+        factor_kernel,
+        out_shape=(
+            jax.ShapeDtypeStruct((n * BINS, n), jnp.float32),
+            jax.ShapeDtypeStruct((BINS, n), jnp.float32),
+        ),
+        in_specs=[pl.BlockSpec(memory_space=pltpu.VMEM)] * 2,
+        out_specs=(pl.BlockSpec(memory_space=pltpu.VMEM), pl.BlockSpec(memory_space=pltpu.VMEM)),
+        scratch_shapes=[pltpu.VMEM((n * BINS, LANES), jnp.float32)] * 2,
+        compiler_params=pltpu.CompilerParams(vmem_limit_bytes=40 * 1024 * 1024),
+    )(flat, steering)
+    return factor.reshape(n, BINS, n), weight
+
+
 def shards(cube, train_blocks, guard_blocks, prior_factor, steering):
+    rows = prior_factor.shape[1]
+    prior = lax.all_gather(prior_factor, "rng", axis=1, tiled=True)
+    prior_gram = forgetting * jnp.einsum(
+        "krd,kre->kde", prior, prior, precision=lax.Precision.HIGHEST
+    )
     table = dft_table(cube.shape[2] * lax.axis_size("dop"))
     pulse_block = lax.all_to_all(cube, "dop", split_axis=3, concat_axis=2, tiled=True)
     spectrum = lax.all_to_all(
@@ -47,27 +164,25 @@
     usable = train_blocks * guard_blocks[None, :]
     gate_mask = jnp.repeat(usable, BLOCK, axis=1).astype(jnp.bfloat16)
     masked = vectors * gate_mask[None, :, :]
+    half = vectors.shape[0] // 2
     gram = jnp.einsum("dkg,ekg->kde", masked, masked, preferred_element_type=jnp.float32)
-    half = vectors.shape[0] // 2
     real_part = gram[:, :half, :half] + gram[:, half:, half:]
     cross = gram[:, half:, :half] - gram[:, :half, half:]
-    prior_gram = forgetting * jnp.einsum(
-        "krd,kre->kde", prior_factor, prior_factor, precision=lax.Precision.HIGHEST
-    )
+    row_id = lax.broadcasted_iota(jnp.int32, (1, half, half), 1)
+    col_id = lax.broadcasted_iota(jnp.int32, (1, half, half), 2)
+    packed = lax.psum(jnp.where(row_id <= col_id, real_part, cross), "rng")
+    flipped = jnp.swapaxes(packed, 1, 2)
+    real_part = jnp.where(row_id <= col_id, packed, flipped)
+    cross = jnp.where(row_id > col_id, packed, jnp.where(row_id < col_id, -flipped, 0.0))
     top = jnp.concatenate([real_part, -cross], axis=2)
     bottom = jnp.concatenate([cross, real_part], axis=2)
-    local = jnp.concatenate([top, bottom], axis=1) + prior_gram
-    covariance = lax.psum(local, "rng")
-    lower = jnp.linalg.cholesky(covariance)
-    first = lax.linalg.triangular_solve(lower, steering[:, :, None], left_side=True, lower=True)
-    second = lax.linalg.triangular_solve(lower, first, left_side=True, lower=True, transpose_a=True)
-    weight = second[:, :, 0] / jnp.sum(first[:, :, 0] * first[:, :, 0], axis=1, keepdims=True)
+    covariance = jnp.concatenate([top, bottom], axis=1) + prior_gram
+    upper, weight = factorize(jnp.swapaxes(covariance, 0, 1), steering)
     rotated = jnp.concatenate([-weight[:, half:], weight[:, :half]], axis=1)
     stacked = jnp.stack([weight, rotated]).astype(jnp.bfloat16)
     filtered = jnp.einsum("skd,dkg->skg", stacked, vectors, preferred_element_type=jnp.float32)
-    rows = prior_factor.shape[1]
     start = lax.axis_index("rng") * rows
-    factor = lax.dynamic_slice_in_dim(jnp.swapaxes(lower, 1, 2), start, rows, axis=1)
+    factor = jnp.swapaxes(lax.dynamic_slice_in_dim(upper, start, rows, axis=0), 0, 1)
     return (filtered, factor)
 
 

time: 742 us -> 435 us (0.59)
  other arithmetic: 434 us -> 4.03 us
  waiting for transfers between devices: 215 us -> 287 us
  Pallas kernels: 0 us -> 66.8 us
  local copies, waits for them, and re-layouts: 44.3 us -> 34.6 us
    another operation x18 -> x2, other arithmetic: 430 us -> 0.01 us  [the longest x10 268 us: shards(): lower = jnp.linalg.cholesky(covariance)]
    all_gather x0 -> x1, waiting for transfers between devices: none -> 78.5 us  [shards(): prior = lax.all_gather(prior_factor, 'rng', axis=1, tiled=True)]
    pallas_call x0 -> x1, Pallas kernels: none -> 66.8 us  [factorize(): pl.pallas_call(factor_kernel, out_shape=(jax.ShapeDtypeStruct((n * BINS,...]
    another operation x8 -> x0, matrix products: 9.37 us -> none  [the longest x2 4.91 us: shards(): lower = jnp.linalg.cholesky(covariance)]
    unnamed x45 -> x29, local copies, waits for them, and re-layouts: 19.4 us -> 16.1 us
  transfers between devices with their start and end apart: 4 -> 5, of which waited for: 3 -> 4; matrix products, arithmetic and copies ran while one was open for 1% -> 2% of each run, Pallas kernels for 0% -> 0%
where the time goes in v1:
time: 435 us; the launch traced here: 431 us
  waiting for transfers between devices  287 us (66%)
  Pallas kernels  66.8 us (15%)
  local copies, waits for them, and re-layouts  34.6 us (8%)
  starting transfers between devices  15.6 us (4%)
  between operations  14.4 us (3%)
  matrix products  8.61 us (2%)
    psum x1, waiting for transfers between devices, shards(): packed = lax.psum(jnp.where(row_id <= col_id, real_part, cross), 'rng')  154 us
    all_gather x1, waiting for transfers between devices, shards(): prior = lax.all_gather(prior_factor, 'rng', axis=1, tiled=True)  78.5 us
    pallas_call x1, Pallas kernels, factorize(): pl.pallas_call(factor_kernel, out_shape=(jax.ShapeDtypeStruct((n * BINS,...  66.8 us
    all_to_all x1, waiting for transfers between devices, shards(): lax.all_to_all(cube, 'dop', split_axis=3, concat_axis=2, tiled=True)  27.4 us
    all_to_all x1, waiting for transfers between devices, shards(): lax.all_to_all(spectra(pulse_block, table), 'dop', split_axis=2, concat_a...  26.8 us
    unnamed x29, local copies, waits for them, and re-layouts  16.1 us
    all_to_all x1, starting transfers between devices, shards(): lax.all_to_all(cube, 'dop', split_axis=3, concat_axis=2, tiled=True)  11.8 us
  transfers between devices with their start and end apart: 5, of which 4 were waited for; matrix products, arithmetic and copies ran while one was open for 2% of the time, Pallas kernels for 0%

profile of v1, /device:TPU:1, one launch (start us, length us, event | category | flops | bytes accessed | tf_op | source)
XLA Modules:
  0.0 431.3 jit_solution(6077556496326421284)
XLA Ops:
  7.2 4.0 copy.35
  11.1 2.3 reshape.126
  13.4 11.8 %all-to-all-start = ((bf16[16,2,16384]{2,1,0:T(2,128)(2,1)}), bf16[16,2,16384]{2,1,0:T(2,128)(2,1)S(1)}, u32[]{:S(2)}, u32[]{:S(2)}) async-start(bf16[16,2,16384]{2,1,0:T(2,128)(2,1)} %reshape.126), calls=%async_computation | async-start | bytes 2097152 | tf_op jit(solution)/shard_map/all_to_all | solution.py:157
  25.8 27.4 %all-to-all-done = bf16[16,2,16384]{2,1,0:T(2,128)(2,1)S(1)} async-done(((bf16[16,2,16384]{2,1,0:T(2,128)(2,1)}), bf16[16,2,16384]{2,1,0:T(2,128)(2,1)S(1)}, u32[]{:S(2)}, u32[]{:S(2)}) %all-to-all-start) | async-done | bytes 1048608 | tf_op jit(solution)/shard_map/all_to_all | solution.py:157
  53.2 1.3 reshape.127
  54.5 1.9 copy.37
  56.4 2.9 copy.38
  60.3 3.0 copy.39
  63.3 2.3 reshape.128
  65.6 3.5 all-to-all-start.1
  70.2 26.8 %all-to-all-done.1 = bf16[16,2,16384]{2,1,0:T(2,128)(2,1)S(1)} async-done(((bf16[16,2,16384]{2,1,0:T(2,128)(2,1)}), bf16[16,2,16384]{2,1,0:T(2,128)(2,1)S(1)}, u32[]{:S(2)}, u32[]{:S(2)}) %all-to-all-start.1) | async-done | bytes 1048608 | tf_op jit(solution)/shard_map/all_to_all | solution.py:158
  97.0 1.3 reshape.129
  98.3 1.7 copy.40
  100.6 1.3 copy-done.1
  102.7 3.2 fusion.29
  106.0 1.5 copy.57
  107.6 1.3 copy.41
  109.7 1.2 fusion.7
  111.0 1.5 fusion.1
  114.2 153.8 %all-reduce.2.cloned.1.call-done = f32[8,128,128]{2,1,0:T(8,128)} async-done(((f32[8,128,128]{2,1,0:T(8,128)}), f32[8,128,128]{2,1,0:T(8,128)}) %all-reduce.2.cloned.1.call-update) | async-done | bytes 524304 | tf_op jit(solution)/shard_map/psum | solution.py:173
  267.9 1.2 copy.48
  270.4 78.5 %all-gather.2.cloned.1.call-done = f32[8,256,256]{2,1,0:T(8,128)} async-done(((f32[8,8,256]{2,1,0:T(8,128)}), f32[8,256,256]{2,1,0:T(8,128)}) %all-gather.2.cloned.1.call-update) | async-done | bytes 2097168 | tf_op jit(solution)/shard_map/all_gather | solution.py:152
  348.9 5.7 %fusion = f32[256,8,256]{2,0,1:T(8,128)S(1)} fusion(f32[8,128,128]{2,1,0:T(8,128)S(1)} %get-tuple-element.16, f32[8,128,128]{2,1,0:T(8,128)S(1)} %get-tuple-element.13, f32[8,128,128]{2,1,0:T(8,128)S(1)} %get-tuple-element.12, f32[8,256,256]{2,1,0:T(8,128)} %all-gather.2.cloned.1.call-done), kind=kOutput, calls=%fused_computation.2 | convolution fusion | flops 1613234176 | bytes 5767168 | tf_op jit(solution)/shard_map/krd,kre->kde/dot_general | solution.py:153
  355.9 66.8 %shard_map.68 = (f32[2048,256]{1,0:T(8,128)S(1)}, f32[8,256]{1,0:T(8,128)S(1)}) custom-call(f32[2048,256]{1,0:T(8,128)S(1)} %bitcast.67, f32[8,256]{1,0:T(8,128)S(1)} %copy-done), custom_call_target="tpu_custom_call" | custom-call | tf_op jit(solution)/shard_map/pallas_call | solution.py:136
  (53 shorter events, 10.6 us)
Async XLA Ops:
  13.4 39.8 %all-to-all-start = ((bf16[16,2,16384]{2,1,0:T(2,128)(2,1)}), bf16[16,2,16384]{2,1,0:T(2,128)(2,1)S(1)}, u32[]{:S(2)}, u32[]{:S(2)}) async-start(bf16[16,2,16384]{2,1,0:T(2,128)(2,1)} %reshape.126), calls=%async_computation | async-start | bytes 2097152 | tf_op jit(solution)/shard_map/all_to_all | solution.py:157
  63.3 6.1 %copy-start.8 = (s32[8,4]{0,1:T(4,128)S(1)}, s32[8,4]{0,1:T(4,128)}, u32[]{:S(2)}) copy-start(s32[8,4]{0,1:T(4,128)} %param.6) | copy-start | bytes 388
  63.3 6.1 %copy-start.9 = (s32[4]{0:T(128)S(1)}, s32[4]{0:T(128)}, u32[]{:S(2)}) copy-start(s32[4]{0:T(128)} %param.7) | copy-start | bytes 52
  65.6 31.4 %all-to-all-start.1 = ((bf16[16,2,16384]{2,1,0:T(2,128)(2,1)}), bf16[16,2,16384]{2,1,0:T(2,128)(2,1)S(1)}, u32[]{:S(2)}, u32[]{:S(2)}) async-start(bf16[16,2,16384]{2,1,0:T(2,128)(2,1)} %reshape.128), calls=%async_computation.1 | async-start | bytes 2097152 | tf_op jit(solution)/shard_map/all_to_all | solution.py:158
  69.1 198.8 %all-reduce.2.cloned.1.call-start = ((), (), s32[]{:S(2)}) async-start(), calls=%async_computation.2 | async-start | bytes 1048576 | tf_op jit(solution)/shard_map/psum | solution.py:173
  100.6 1.3 copy-start.1
  102.7 7.0 %collective-permute-start = (bf16[2,64,1,512]{3,1,2,0:T(8,128)(2,1)}, bf16[2,64,1,512]{3,1,2,0:T(8,128)(2,1)S(1)}, u32[]{:S(2)}, u32[]{:S(2)}) collective-permute-start(bf16[2,64,1,512]{3,1,2,0:T(8,128)(2,1)} %copy.58), channel_id=1, source_target_pairs={{32,0},{64,32},{96,64},{128,96},{160,128},{192,160},{224,192},{256... | collective-permute-start | bytes 393224 | tf_op jit(solution)/shard_map/ppermute | solution.py:21
  102.7 3.2 copy-start.2
  109.3 1.6 copy-start.7
  110.9 1.5 copy-start.3
  111.0 1.5 copy-start.5
  113.4 235.5 %all-gather.2.cloned.1.call-start = ((), (), s32[]{:S(2)}) async-start(), calls=%async_computation.3 | async-start | bytes 2162688 | tf_op jit(solution)/shard_map/all_gather | solution.py:152
  354.6 1.3 copy-start
  355.9 67.6 %copy-start.4 = (bf16[64,8,512]{2,0,1:T(8,128)(2,1)S(1)}, bf16[64,8,512]{2,0,1:T(8,128)(2,1)}, u32[]{:S(2)}) copy-start(bf16[64,8,512]{2,0,1:T(8,128)(2,1)} %copy-done.3) | copy-start | bytes 1572868
  355.9 67.6 %copy-start.6 = (bf16[64,8,512]{2,0,1:T(8,128)(2,1)S(1)}, bf16[64,8,512]{2,0,1:T(8,128)(2,1)}, u32[]{:S(2)}) copy-start(bf16[64,8,512]{2,0,1:T(8,128)(2,1)} %copy-done.5) | copy-start | bytes 1572868
Sparse Core Ops, SparseCore 0:
  113.5 154.3 all-reduce.1
  271.0 77.8 all-gather.1

commit v2 on v1

--- a/solution.py
+++ b/solution.py
@@ -1,3 +1,4 @@
+import functools
 import math
 
 import jax
@@ -130,6 +131,90 @@
         weight_ref[:, c * LANES : (c + 1) * LANES] = q[c] / vv
 
 
+def sum_kernel(n, part_ref, out_ref, slots, send1, recv1, send2, recv2):
+    me = lax.axis_index("rng")
+    row = lax.axis_index("dop")
+
+    def other(d):
+        return lax.rem(me + d, n)
+
+    def source(d):
+        return lax.rem(me + n - d, n)
+
+    barrier = pltpu.get_barrier_semaphore()
+
+    def greet(d, _):
+        pl.semaphore_signal(
+            barrier, inc=1, device_id=(row, other(d)), device_id_type=pl.DeviceIdType.MESH
+        )
+        return 0
+
+    lax.fori_loop(1, n, greet, 0)
+    pl.semaphore_wait(barrier, n - 1)
+
+    def scatter(d):
+        return pltpu.make_async_remote_copy(
+            src_ref=part_ref.at[other(d)],
+            dst_ref=slots.at[d],
+            send_sem=send1.at[d],
+            recv_sem=recv1.at[d],
+            device_id=(row, other(d)),
+            device_id_type=pl.DeviceIdType.MESH,
+        )
+
+    def spread(d, chunk):
+        return pltpu.make_async_remote_copy(
+            src_ref=out_ref.at[chunk],
+            dst_ref=out_ref.at[chunk],
+            send_sem=send2.at[d],
+            recv_sem=recv2.at[d],
+            device_id=(row, other(d)),
+            device_id_type=pl.DeviceIdType.MESH,
+        )
+
+    def start_scatter(d, _):
+        scatter(d).start()
+        return 0
+
+    lax.fori_loop(1, n, start_scatter, 0)
+
+    def add(d, total):
+        scatter(d).wait_recv()
+        return total + slots[d]
+
+    out_ref[me] = lax.fori_loop(1, n, add, part_ref[me])
+
+    def start_spread(d, _):
+        spread(d, me).start()
+        return 0
+
+    lax.fori_loop(1, n, start_spread, 0)
+
+    def finish(d, _):
+        scatter(d).wait_send()
+        spread(d, me).wait_send()
+        spread(d, source(d)).wait_recv()
+        return 0
+
+    lax.fori_loop(1, n, finish, 0)
+
+
+def sum_over_rng(part):
+    n = lax.axis_size("rng")
+    chunks = part.reshape(n, -1, LANES)
+    size = chunks.shape[1]
+    total = pl.pallas_call(
+        functools.partial(sum_kernel, n),
+        out_shape=jax.ShapeDtypeStruct(chunks.shape, jnp.float32),
+        in_specs=[pl.BlockSpec(memory_space=pltpu.VMEM)],
+        out_specs=pl.BlockSpec(memory_space=pltpu.VMEM),
+        scratch_shapes=[pltpu.VMEM((n, size, LANES), jnp.float32)]
+        + [pltpu.SemaphoreType.DMA((n,))] * 4,
+        compiler_params=pltpu.CompilerParams(collective_id=0, has_side_effects=True),
+    )(chunks)
+    return total.reshape(part.shape)
+
+
 def factorize(covariance, steering):
     n = covariance.shape[0]
     flat = covariance.reshape(n * BINS, n)
@@ -150,14 +235,12 @@
 def shards(cube, train_blocks, guard_blocks, prior_factor, steering):
     rows = prior_factor.shape[1]
     prior = lax.all_gather(prior_factor, "rng", axis=1, tiled=True)
-    prior_gram = forgetting * jnp.einsum(
-        "krd,kre->kde", prior, prior, precision=lax.Precision.HIGHEST
-    )
     table = dft_table(cube.shape[2] * lax.axis_size("dop"))
     pulse_block = lax.all_to_all(cube, "dop", split_axis=3, concat_axis=2, tiled=True)
     spectrum = lax.all_to_all(
         spectra(pulse_block, table), "dop", split_axis=2, concat_axis=3, tiled=True
     )
+    spectrum, prior = lax.optimization_barrier((spectrum, prior))
     neighbor = from_behind(spectrum[:, :, 0:1, :], "dop", -1)
     following = jnp.concatenate([spectrum[:, :, 1:, :], neighbor], axis=2)
     vectors = jnp.concatenate([spectrum[0], following[0], spectrum[1], following[1]], axis=0)
@@ -170,7 +253,10 @@
     cross = gram[:, half:, :half] - gram[:, :half, half:]
     row_id = lax.broadcasted_iota(jnp.int32, (1, half, half), 1)
     col_id = lax.broadcasted_iota(jnp.int32, (1, half, half), 2)
-    packed = lax.psum(jnp.where(row_id <= col_id, real_part, cross), "rng")
+    prior_gram = forgetting * jnp.einsum(
+        "krd,kre->kde", prior, prior, precision=lax.Precision.HIGHEST
+    )
+    packed = sum_over_rng(jnp.where(row_id <= col_id, real_part, cross))
     flipped = jnp.swapaxes(packed, 1, 2)
     real_part = jnp.where(row_id <= col_id, packed, flipped)
     cross = jnp.where(row_id > col_id, packed, jnp.where(row_id < col_id, -flipped, 0.0))

time: 435 us -> 238 us (0.55)
  waiting for transfers between devices: 287 us -> 63.4 us
  Pallas kernels: 66.8 us -> 104 us
  local copies, waits for them, and re-layouts: 34.6 us -> 27 us
    psum x1 -> x0, waiting for transfers between devices: 154 us -> none  [shards(): packed = lax.psum(jnp.where(row_id <= col_id, real_part, cross), 'rng')]
    all_gather x1, waiting for transfers between devices: 78.5 us -> 5 us  [shards(): prior = lax.all_gather(prior_factor, 'rng', axis=1, tiled=True)]
    pallas_call x0 -> x1, Pallas kernels: none -> 37.6 us  [sum_over_rng(): pl.pallas_call(functools.partial(sum_kernel, n), out_shape=jax.ShapeDtype...]
    slice x3 -> x0, local copies, waits for them, and re-layouts: 4.59 us -> none  [the longest x2 4.5 us: shards(): spectrum[0]]
    unnamed x29 -> x27, local copies, waits for them, and re-layouts: 16.1 us -> 13.4 us
  transfers between devices with their start and end apart: 5 -> 4, of which waited for: 4 -> 4; matrix products, arithmetic and copies ran while one was open for 2% -> 7% of each run, Pallas kernels for 0% -> 0%
where the time goes in v2:
time: 238 us
  Pallas kernels  104 us (44%)
  waiting for transfers between devices  63.4 us (27%)
  local copies, waits for them, and re-layouts  27 us (11%)
  starting transfers between devices  19.4 us (8%)
  between operations  14.4 us (6%)
  matrix products  6.34 us (3%)
  other arithmetic  2.88 us (1%)
    pallas_call x1, Pallas kernels, factorize(): pl.pallas_call(factor_kernel, out_shape=(jax.ShapeDtypeStruct((n * BINS,...  66.8 us
    pallas_call x1, Pallas kernels, sum_over_rng(): pl.pallas_call(functools.partial(sum_kernel, n), out_shape=jax.ShapeDtype...  37.6 us
    all_to_all x1, waiting for transfers between devices, shards(): lax.all_to_all(spectra(pulse_block, table), 'dop', split_axis=2, concat_a...  27.4 us
    all_to_all x1, waiting for transfers between devices, shards(): lax.all_to_all(cube, 'dop', split_axis=3, concat_axis=2, tiled=True)  26.7 us
    unnamed x27, local copies, waits for them, and re-layouts  13.4 us
    all_to_all x1, starting transfers between devices, shards(): lax.all_to_all(cube, 'dop', split_axis=3, concat_axis=2, tiled=True)  11.8 us
    all_gather x1, waiting for transfers between devices, shards(): prior = lax.all_gather(prior_factor, 'rng', axis=1, tiled=True)  5 us
  transfers between devices with their start and end apart: 4, of which 4 were waited for; matrix products, arithmetic and copies ran while one was open for 7% of the time, Pallas kernels for 0%

profile of v2, /device:TPU:1, one launch (start us, length us, event | category | flops | bytes accessed | tf_op | source)
XLA Modules:
  0.0 237.8 jit_solution(4341218353228555818)
XLA Ops:
  7.2 4.0 %copy.33 = bf16[2,64,8,512]{1,2,0,3:T(8,128)(2,1)S(1)} copy(bf16[2,64,8,512]{3,2,1,0:T(8,128)(2,1)} %param.5) | data formatting | bytes 2097152 | tf_op args[0]
  11.1 2.3 reshape.130
  13.4 11.8 %all-to-all-start = ((bf16[16,2,16384]{2,1,0:T(2,128)(2,1)}), bf16[16,2,16384]{2,1,0:T(2,128)(2,1)S(1)}, u32[]{:S(2)}, u32[]{:S(2)}) async-start(bf16[16,2,16384]{2,1,0:T(2,128)(2,1)} %reshape.130), calls=%async_computation | async-start | bytes 2097152 | tf_op jit(solution)/shard_map/all_to_all | solution.py:239
  26.5 26.7 %all-to-all-done = bf16[16,2,16384]{2,1,0:T(2,128)(2,1)S(1)} async-done(((bf16[16,2,16384]{2,1,0:T(2,128)(2,1)}), bf16[16,2,16384]{2,1,0:T(2,128)(2,1)S(1)}, u32[]{:S(2)}, u32[]{:S(2)}) %all-to-all-start) | async-done | bytes 1048608 | tf_op jit(solution)/shard_map/all_to_all | solution.py:239
  53.2 1.3 reshape.131
  54.5 1.8 copy.35
  56.4 2.9 %copy.36 = bf16[2,64,128,32]{2,1,0,3:T(8,128)(2,1)S(1)} copy(bf16[2,64,128,32]{1,3,2,0:T(8,128)(2,1)} %bitcast.79) | data formatting | bytes 2097152 | tf_op jit(solution)/shard_map/all_to_all | solution.py:239
  59.3 1.0 fusion.3
  60.3 3.0 %copy.37 = bf16[2,64,128,32]{1,3,0,2:T(8,128)(2,1)S(1)} copy(bf16[2,64,128,32]{2,1,3,0:T(8,128)(2,1)S(1)} %fusion.3) | data formatting | bytes 2097152 | tf_op jit(solution)/shard_map/convert_element_type | solution.py:40
  63.3 2.3 reshape.132
  65.6 3.7 %all-to-all-start.1 = ((bf16[16,2,16384]{2,1,0:T(2,128)(2,1)}), bf16[16,2,16384]{2,1,0:T(2,128)(2,1)S(1)}, u32[]{:S(2)}, u32[]{:S(2)}) async-start(bf16[16,2,16384]{2,1,0:T(2,128)(2,1)} %reshape.132), calls=%async_computation.1 | async-start | bytes 2097152 | tf_op jit(solution)/shard_map/all_to_all | solution.py:240
  69.5 27.4 %all-to-all-done.1 = bf16[16,2,16384]{2,1,0:T(2,128)(2,1)S(1)} async-done(((bf16[16,2,16384]{2,1,0:T(2,128)(2,1)}), bf16[16,2,16384]{2,1,0:T(2,128)(2,1)S(1)}, u32[]{:S(2)}, u32[]{:S(2)}) %all-to-all-start.1) | async-done | bytes 1048608 | tf_op jit(solution)/shard_map/all_to_all | solution.py:240
  96.9 2.3 reshape.133
  99.2 2.1 copy.39
  101.4 5.0 %all-gather.2.cloned.1.call-done = f32[8,256,256]{2,1,0:T(8,128)} async-done(((f32[8,8,256]{2,1,0:T(8,128)}), f32[8,256,256]{2,1,0:T(8,128)}) %all-gather.2.cloned.1.call-update) | async-done | bytes 2097168 | tf_op jit(solution)/shard_map/all_gather | solution.py:237
  107.2 3.8 %collective-permute-start = (bf16[2,64,1,512]{3,1,2,0:T(8,128)(2,1)S(1)}, bf16[2,64,1,512]{3,1,2,0:T(8,128)(2,1)S(1)}, u32[]{:S(2)}, u32[]{:S(2)}) collective-permute-start(bf16[2,64,1,512]{3,1,2,0:T(8,128)(2,1)S(1)} %slice.51), channel_id=1, source_target_pairs={{32,0},{64,32},{96,64},{128,96},{160,128},{192,160},{224,192},{256... | collective-permute-start | bytes 393224 | tf_op jit(solution)/shard_map/ppermute | solution.py:22
  111.2 3.6 %collective-permute-done = bf16[2,64,1,512]{3,1,2,0:T(8,128)(2,1)S(1)} collective-permute-done((bf16[2,64,1,512]{3,1,2,0:T(8,128)(2,1)S(1)}, bf16[2,64,1,512]{3,1,2,0:T(8,128)(2,1)S(1)}, u32[]{:S(2)}, u32[]{:S(2)}) %collective-permute-start) | collective-permute-done | bytes 131104 | tf_op jit(solution)/shard_map/ppermute | solution.py:22
  115.0 1.5 fusion.1
  117.4 37.6 %shard_map.68 = f32[32,32,128]{2,1,0:T(8,128)} custom-call(f32[32,32,128]{2,1,0:T(8,128)} %bitcast.83), custom_call_target="tpu_custom_call" | custom-call | tf_op jit(solution)/shard_map/pallas_call | solution.py:206
  155.0 1.4 copy.44
  156.4 1.2 fusion.27
  157.6 3.5 %fusion = f32[256,8,256]{2,0,1:T(8,128)S(1)} fusion(f32[8,128,128]{2,1,0:T(8,128)S(1)} %get-tuple-element.18, f32[8,128,128]{2,1,0:T(8,128)S(1)} %get-tuple-element.17, f32[8,128,128]{2,1,0:T(8,128)S(1)} %get-tuple-element.16, f32[8,256,256]{2,1,0:T(8,128)S(1)} %copy-done.1), kind=kOutput, calls=%fused_computation.2 | convolution fusion | flops 1613234176 | bytes 5767168 | tf_op jit(solution)/shard_map/krd,kre->kde/dot_general | solution.py:256
  161.2 1.2 copy.60
  162.4 66.8 %shard_map.69 = (f32[2048,256]{1,0:T(8,128)S(1)}, f32[8,256]{1,0:T(8,128)S(1)}) custom-call(f32[2048,256]{1,0:T(8,128)S(1)} %bitcast.73, f32[8,256]{1,0:T(8,128)S(1)} %copy-done), custom_call_target="tpu_custom_call" | custom-call | tf_op jit(solution)/shard_map/pallas_call | solution.py:221
  (45 shorter events, 5.2 us)
Async XLA Ops:
  13.4 39.8 %all-to-all-start = ((bf16[16,2,16384]{2,1,0:T(2,128)(2,1)}), bf16[16,2,16384]{2,1,0:T(2,128)(2,1)S(1)}, u32[]{:S(2)}, u32[]{:S(2)}) async-start(bf16[16,2,16384]{2,1,0:T(2,128)(2,1)} %reshape.130), calls=%async_computation | async-start | bytes 2097152 | tf_op jit(solution)/shard_map/all_to_all | solution.py:239
  25.2 81.2 %all-gather.2.cloned.1.call-start = ((), (), s32[]{:S(2)}) async-start(), calls=%async_computation.2 | async-start | bytes 2162688 | tf_op jit(solution)/shard_map/all_gather | solution.py:237
  63.3 6.1 %copy-start.8 = (s32[8,4]{0,1:T(4,128)S(1)}, s32[8,4]{0,1:T(4,128)}, u32[]{:S(2)}) copy-start(s32[8,4]{0,1:T(4,128)} %param.6) | copy-start | bytes 388
  63.3 6.1 %copy-start.9 = (s32[4]{0:T(128)S(1)}, s32[4]{0:T(128)}, u32[]{:S(2)}) copy-start(s32[4]{0:T(128)} %param.7) | copy-start | bytes 52
  65.6 31.3 %all-to-all-start.1 = ((bf16[16,2,16384]{2,1,0:T(2,128)(2,1)}), bf16[16,2,16384]{2,1,0:T(2,128)(2,1)S(1)}, u32[]{:S(2)}, u32[]{:S(2)}) async-start(bf16[16,2,16384]{2,1,0:T(2,128)(2,1)} %reshape.132), calls=%async_computation.1 | async-start | bytes 2097152 | tf_op jit(solution)/shard_map/all_to_all | solution.py:240
  107.2 7.7 %collective-permute-start = (bf16[2,64,1,512]{3,1,2,0:T(8,128)(2,1)S(1)}, bf16[2,64,1,512]{3,1,2,0:T(8,128)(2,1)S(1)}, u32[]{:S(2)}, u32[]{:S(2)}) collective-permute-start(bf16[2,64,1,512]{3,1,2,0:T(8,128)(2,1)S(1)} %slice.51), channel_id=1, source_target_pairs={{32,0},{64,32},{96,64},{128,96},{160,128},{192,160},{224,192},{256... | collective-permute-start | bytes 393224 | tf_op jit(solution)/shard_map/ppermute | solution.py:22
  111.2 5.3 %copy-start.2 = (bf16[64,8,512]{2,0,1:T(8,128)(2,1)}, bf16[64,8,512]{2,0,1:T(8,128)(2,1)S(1)}, u32[]{:S(2)}) copy-start(bf16[64,8,512]{2,0,1:T(8,128)(2,1)S(1)} %get-tuple-element.20) | copy-start | bytes 1572868
  115.0 1.5 copy-start.4
  115.0 1.5 copy-start.6
  155.0 2.6 %copy-start.1 = (f32[8,256,256]{2,1,0:T(8,128)S(1)}, f32[8,256,256]{2,1,0:T(8,128)}, u32[]{:S(2)}) copy-start(f32[8,256,256]{2,1,0:T(8,128)} %all-gather.2.cloned.1.call-done) | copy-start | bytes 6291460
  161.1 1.3 copy-start
  162.4 67.6 %copy-start.3 = (bf16[64,8,512]{2,0,1:T(8,128)(2,1)S(1)}, bf16[64,8,512]{2,0,1:T(8,128)(2,1)}, u32[]{:S(2)}) copy-start(bf16[64,8,512]{2,0,1:T(8,128)(2,1)} %copy-done.2) | copy-start | bytes 1572868
  162.4 67.6 %copy-start.5 = (bf16[64,8,512]{2,0,1:T(8,128)(2,1)S(1)}, bf16[64,8,512]{2,0,1:T(8,128)(2,1)}, u32[]{:S(2)}) copy-start(bf16[64,8,512]{2,0,1:T(8,128)(2,1)} %copy-done.4) | copy-start | bytes 1572868
  162.4 67.6 %copy-start.7 = (bf16[64,8,512]{2,0,1:T(8,128)(2,1)S(1)}, bf16[64,8,512]{2,0,1:T(8,128)(2,1)}, u32[]{:S(2)}) copy-start(bf16[64,8,512]{2,0,1:T(8,128)(2,1)} %copy-done.6) | copy-start | bytes 1572868
Sparse Core Ops, SparseCore 0:
  29.1 77.2 all-gather.1

commit v3 on v1

--- a/solution.py
+++ b/solution.py
@@ -1,3 +1,4 @@
+import functools
 import math
 
 import jax
@@ -11,6 +12,7 @@
 BINS = 8
 LANES = 128
 PANEL = 8
+COLUMN = 8
 
 forgetting = 0.98
 
@@ -58,23 +60,29 @@
         o = p * PANEL
         base = h * LANES + o
         pair = [[halves[c][rows(base + i), :] for c in range(2)] for i in range(PANEL)]
+        block = [[lane(pair[j][h], o + i) if i >= j else None for i in range(PANEL)] for j in range(PANEL)]
+        side = [lane(s[h], o + j) for j in range(PANEL)]
         final = []
         for j in range(PANEL):
             own = at == o + j
-            pivot = lane(pair[j][h], o + j)
+            pivot = block[j][j]
             inv = lax.rsqrt(pivot)
             inv2 = inv * inv
+            ratio = [block[j][i] * inv2 if i > j else None for i in range(PANEL)]
+            for i in range(j + 1, PANEL):
+                for l in range(i, PANEL):
+                    block[i][l] = block[i][l] - ratio[i] * block[j][l]
+                side[i] = side[i] - ratio[i] * side[j]
             source = list(pair[j])
             source[h] = jnp.where(own, 1.0, source[h])
             for i in range(j + 1, PANEL):
-                m = lane(pair[j][h], o + i) * inv2
                 target = list(pair[i])
                 target[h] = jnp.where(own, 0.0, target[h])
-                pair[i] = [target[c] - m * source[c] for c in range(2)]
+                pair[i] = [target[c] - ratio[i] * source[c] for c in range(2)]
             row = [source[c] * inv for c in range(2)]
-            v = lane(s[h], o + j) * inv
+            v = side[j] * inv
             s = [s[c] - v * row[c] for c in range(2)]
-            below = [row[0], jnp.zeros_like(row[1])] if h else [row[0], jnp.zeros_like(row[1])]
+            below = [row[0], jnp.zeros_like(row[1])]
             below[h] = jnp.where(at <= o + j, row[h], 0.0)
             q = [q[c] + v * below[c] for c in range(2)]
             vv = vv + v * v
@@ -128,6 +136,106 @@
     s, q, vv = lax.fori_loop(0, LANES // PANEL, lambda p, c: panel(1, p, c), carry)
     for c in range(2):
         weight_ref[:, c * LANES : (c + 1) * LANES] = q[c] / vv
+
+
+def sum_kernel(nx, ny, part_ref, out_ref, slots_x, held, slots_y, sends, arrivals):
+    me = lax.axis_index("rng")
+    row = lax.axis_index("dop")
+    x = me // ny
+    y = lax.rem(me, ny)
+
+    def along_x(d):
+        return (row, lax.rem(x + d, nx) * ny + y)
+
+    def along_y(d):
+        return (row, x * ny + lax.rem(y + d, ny))
+
+    barrier = pltpu.get_barrier_semaphore()
+    for d in range(1, nx):
+        pl.semaphore_signal(
+            barrier, inc=1, device_id=along_x(d), device_id_type=pl.DeviceIdType.MESH
+        )
+    for d in range(1, ny):
+        pl.semaphore_signal(
+            barrier, inc=1, device_id=along_y(d), device_id_type=pl.DeviceIdType.MESH
+        )
+    pl.semaphore_wait(barrier, nx + ny - 2)
+
+    def copy(source, target, stage, d, device):
+        return pltpu.make_async_remote_copy(
+            src_ref=source,
+            dst_ref=target,
+            send_sem=sends.at[stage, d],
+            recv_sem=arrivals.at[stage, d],
+            device_id=device,
+            device_id_type=pl.DeviceIdType.MESH,
+        )
+
+    def scatter_x(d):
+        return copy(part_ref.at[lax.rem(x + d, nx)], slots_x.at[d], 0, d, along_x(d))
+
+    def scatter_y(d):
+        return copy(held.at[lax.rem(y + d, ny)], slots_y.at[d], 1, d, along_y(d))
+
+    def gather_y(d, place):
+        return copy(out_ref.at[x, place], out_ref.at[x, place], 2, d, along_y(d))
+
+    def gather_x(d, place):
+        return copy(out_ref.at[place], out_ref.at[place], 3, d, along_x(d))
+
+    for d in range(1, nx):
+        scatter_x(d).start()
+    for d in range(1, nx):
+        scatter_x(d).wait_recv()
+    total = part_ref[x]
+    for d in range(1, nx):
+        total = total + slots_x[d]
+    held[...] = total
+    for d in range(1, ny):
+        scatter_y(d).start()
+    for d in range(1, ny):
+        scatter_y(d).wait_recv()
+    total = held[y]
+    for d in range(1, ny):
+        total = total + slots_y[d]
+    out_ref[x, y] = total
+    for d in range(1, ny):
+        gather_y(d, y).start()
+    for d in range(1, ny):
+        gather_y(d, lax.rem(y + ny - d, ny)).wait_recv()
+    for d in range(1, nx):
+        gather_x(d, x).start()
+    for d in range(1, nx):
+        gather_x(d, lax.rem(x + nx - d, nx)).wait_recv()
+    for d in range(1, nx):
+        scatter_x(d).wait_send()
+        gather_x(d, x).wait_send()
+    for d in range(1, ny):
+        scatter_y(d).wait_send()
+        gather_y(d, y).wait_send()
+
+
+def sum_over_rng(part):
+    n = lax.axis_size("rng")
+    ny = COLUMN
+    nx = n // ny
+    chunks = part.reshape(nx, ny, -1, LANES)
+    size = chunks.shape[2]
+    total = pl.pallas_call(
+        functools.partial(sum_kernel, nx, ny),
+        out_shape=jax.ShapeDtypeStruct(chunks.shape, jnp.float32),
+        in_specs=[pl.BlockSpec(memory_space=pltpu.VMEM)],
+        out_specs=pl.BlockSpec(memory_space=pltpu.VMEM),
+        scratch_shapes=[
+            pltpu.VMEM((nx, ny, size, LANES), jnp.float32),
+            pltpu.VMEM((ny, size, LANES), jnp.float32),
+            pltpu.VMEM((ny, size, LANES), jnp.float32),
+            pltpu.SemaphoreType.DMA((4, ny)),
+            pltpu.SemaphoreType.DMA((4, ny)),
+        ],
+        compiler_params=pltpu.CompilerParams(collective_id=0, has_side_effects=True),
+    )(chunks)
+    return total.reshape(part.shape)
 
 
 def factorize(covariance, steering):
@@ -150,14 +258,12 @@
 def shards(cube, train_blocks, guard_blocks, prior_factor, steering):
     rows = prior_factor.shape[1]
     prior = lax.all_gather(prior_factor, "rng", axis=1, tiled=True)
-    prior_gram = forgetting * jnp.einsum(
-        "krd,kre->kde", prior, prior, precision=lax.Precision.HIGHEST
-    )
     table = dft_table(cube.shape[2] * lax.axis_size("dop"))
     pulse_block = lax.all_to_all(cube, "dop", split_axis=3, concat_axis=2, tiled=True)
     spectrum = lax.all_to_all(
         spectra(pulse_block, table), "dop", split_axis=2, concat_axis=3, tiled=True
     )
+    spectrum, prior = lax.optimization_barrier((spectrum, prior))
     neighbor = from_behind(spectrum[:, :, 0:1, :], "dop", -1)
     following = jnp.concatenate([spectrum[:, :, 1:, :], neighbor], axis=2)
     vectors = jnp.concatenate([spectrum[0], following[0], spectrum[1], following[1]], axis=0)
@@ -170,7 +276,10 @@
     cross = gram[:, half:, :half] - gram[:, :half, half:]
     row_id = lax.broadcasted_iota(jnp.int32, (1, half, half), 1)
     col_id = lax.broadcasted_iota(jnp.int32, (1, half, half), 2)
-    packed = lax.psum(jnp.where(row_id <= col_id, real_part, cross), "rng")
+    prior_gram = forgetting * jnp.einsum(
+        "krd,kre->kde", prior, prior, precision=lax.Precision.HIGHEST
+    )
+    packed = sum_over_rng(jnp.where(row_id <= col_id, real_part, cross))
     flipped = jnp.swapaxes(packed, 1, 2)
     real_part = jnp.where(row_id <= col_id, packed, flipped)
     cross = jnp.where(row_id > col_id, packed, jnp.where(row_id < col_id, -flipped, 0.0))

time: 435 us -> 218 us (0.50)
  waiting for transfers between devices: 287 us -> 63.4 us
  Pallas kernels: 66.8 us -> 82.7 us
  local copies, waits for them, and re-layouts: 34.6 us -> 27 us
    psum x1 -> x0, waiting for transfers between devices: 154 us -> none  [shards(): packed = lax.psum(jnp.where(row_id <= col_id, real_part, cross), 'rng')]
    all_gather x1, waiting for transfers between devices: 78.5 us -> 5 us  [shards(): prior = lax.all_gather(prior_factor, 'rng', axis=1, tiled=True)]
    pallas_call x0 -> x1, Pallas kernels: none -> 31.5 us  [sum_over_rng(): pl.pallas_call(functools.partial(sum_kernel, nx, ny), out_shape=jax.Shape...]
    pallas_call x1, Pallas kernels: 66.8 us -> 51.2 us  [factorize(): pl.pallas_call(factor_kernel, out_shape=(jax.ShapeDtypeStruct((n * BINS,...]
    slice x3 -> x0, local copies, waits for them, and re-layouts: 4.59 us -> none  [the longest x2 4.5 us: shards(): spectrum[0]]
    unnamed x29 -> x27, local copies, waits for them, and re-layouts: 16.1 us -> 13.4 us
  transfers between devices with their start and end apart: 5 -> 4, of which waited for: 4 -> 4; matrix products, arithmetic and copies ran while one was open for 2% -> 8% of each run, Pallas kernels for 0% -> 0%
where the time goes in v3:
time: 218 us; the launch traced here: 216 us
  Pallas kernels  82.7 us (38%)
  waiting for transfers between devices  63.4 us (29%)
  local copies, waits for them, and re-layouts  27 us (12%)
  starting transfers between devices  19.4 us (9%)
  between operations  14.4 us (7%)
  matrix products  6.34 us (3%)
  other arithmetic  2.88 us (1%)
    pallas_call x1, Pallas kernels, factorize(): pl.pallas_call(factor_kernel, out_shape=(jax.ShapeDtypeStruct((n * BINS,...  51.2 us
    pallas_call x1, Pallas kernels, sum_over_rng(): pl.pallas_call(functools.partial(sum_kernel, nx, ny), out_shape=jax.Shape...  31.5 us
    all_to_all x1, waiting for transfers between devices, shards(): lax.all_to_all(spectra(pulse_block, table), 'dop', split_axis=2, concat_a...  27.4 us
    all_to_all x1, waiting for transfers between devices, shards(): lax.all_to_all(cube, 'dop', split_axis=3, concat_axis=2, tiled=True)  26.7 us
    unnamed x27, local copies, waits for them, and re-layouts  13.4 us
    all_to_all x1, starting transfers between devices, shards(): lax.all_to_all(cube, 'dop', split_axis=3, concat_axis=2, tiled=True)  11.8 us
    all_gather x1, waiting for transfers between devices, shards(): prior = lax.all_gather(prior_factor, 'rng', axis=1, tiled=True)  5 us
    all_to_all x2, local copies, waits for them, and re-layouts, shards(): lax.all_to_all(cube, 'dop', split_axis=3, concat_axis=2, tiled=True)  4.72 us
  transfers between devices with their start and end apart: 4, of which 4 were waited for; matrix products, arithmetic and copies ran while one was open for 8% of the time, Pallas kernels for 0%

profile of v3, /device:TPU:1, one launch (start us, length us, event | category | flops | bytes accessed | tf_op | source)
XLA Modules:
  0.0 216.1 jit_solution(16895626107605196673)
XLA Ops:
  7.2 4.0 %copy.33 = bf16[2,64,8,512]{1,2,0,3:T(8,128)(2,1)S(1)} copy(bf16[2,64,8,512]{3,2,1,0:T(8,128)(2,1)} %param.5) | data formatting | bytes 2097152 | tf_op args[0]
  11.1 2.3 %reshape.130 = bf16[16,2,16384]{2,1,0:T(2,128)(2,1)} reshape(bf16[512,2,8,64]{3,2,1,0:T(8,128)(2,1)S(1)} %bitcast.73) | data formatting | bytes 2097152
  13.4 11.8 %all-to-all-start = ((bf16[16,2,16384]{2,1,0:T(2,128)(2,1)}), bf16[16,2,16384]{2,1,0:T(2,128)(2,1)S(1)}, u32[]{:S(2)}, u32[]{:S(2)}) async-start(bf16[16,2,16384]{2,1,0:T(2,128)(2,1)} %reshape.130), calls=%async_computation | async-start | bytes 2097152 | tf_op jit(solution)/shard_map/all_to_all | solution.py:262
  26.5 26.7 %all-to-all-done = bf16[16,2,16384]{2,1,0:T(2,128)(2,1)S(1)} async-done(((bf16[16,2,16384]{2,1,0:T(2,128)(2,1)}), bf16[16,2,16384]{2,1,0:T(2,128)(2,1)S(1)}, u32[]{:S(2)}, u32[]{:S(2)}) %all-to-all-start) | async-done | bytes 1048608 | tf_op jit(solution)/shard_map/all_to_all | solution.py:262
  53.2 1.3 reshape.131
  54.5 1.8 copy.35
  56.4 2.9 %copy.36 = bf16[2,64,128,32]{2,1,0,3:T(8,128)(2,1)S(1)} copy(bf16[2,64,128,32]{1,3,2,0:T(8,128)(2,1)} %bitcast.76) | data formatting | bytes 2097152 | tf_op jit(solution)/shard_map/all_to_all | solution.py:262
  59.3 1.0 fusion.3
  60.3 3.0 %copy.37 = bf16[2,64,128,32]{1,3,0,2:T(8,128)(2,1)S(1)} copy(bf16[2,64,128,32]{2,1,3,0:T(8,128)(2,1)S(1)} %fusion.3) | data formatting | bytes 2097152 | tf_op jit(solution)/shard_map/convert_element_type | solution.py:41
  63.3 2.3 %reshape.132 = bf16[16,2,16384]{2,1,0:T(2,128)(2,1)} reshape(bf16[128,2,32,64]{3,2,1,0:T(8,128)(2,1)S(1)} %bitcast.72) | data formatting | bytes 2097152
  65.6 3.7 %all-to-all-start.1 = ((bf16[16,2,16384]{2,1,0:T(2,128)(2,1)}), bf16[16,2,16384]{2,1,0:T(2,128)(2,1)S(1)}, u32[]{:S(2)}, u32[]{:S(2)}) async-start(bf16[16,2,16384]{2,1,0:T(2,128)(2,1)} %reshape.132), calls=%async_computation.1 | async-start | bytes 2097152 | tf_op jit(solution)/shard_map/all_to_all | solution.py:263
  69.5 27.4 %all-to-all-done.1 = bf16[16,2,16384]{2,1,0:T(2,128)(2,1)S(1)} async-done(((bf16[16,2,16384]{2,1,0:T(2,128)(2,1)}), bf16[16,2,16384]{2,1,0:T(2,128)(2,1)S(1)}, u32[]{:S(2)}, u32[]{:S(2)}) %all-to-all-start.1) | async-done | bytes 1048608 | tf_op jit(solution)/shard_map/all_to_all | solution.py:263
  96.9 2.3 %reshape.133 = bf16[128,2,32,64]{3,2,1,0:T(8,128)(2,1)} reshape(bf16[16,2,16384]{2,1,0:T(2,128)(2,1)S(1)} %all-to-all-done.1) | data formatting | bytes 2097152
  99.2 2.1 copy.39
  101.4 5.0 %all-gather.2.cloned.1.call-done = f32[8,256,256]{2,1,0:T(8,128)} async-done(((f32[8,8,256]{2,1,0:T(8,128)}), f32[8,256,256]{2,1,0:T(8,128)}) %all-gather.2.cloned.1.call-update) | async-done | bytes 2097168 | tf_op jit(solution)/shard_map/all_gather | solution.py:260
  107.2 3.8 %collective-permute-start = (bf16[2,64,1,512]{3,1,2,0:T(8,128)(2,1)S(1)}, bf16[2,64,1,512]{3,1,2,0:T(8,128)(2,1)S(1)}, u32[]{:S(2)}, u32[]{:S(2)}) collective-permute-start(bf16[2,64,1,512]{3,1,2,0:T(8,128)(2,1)S(1)} %slice.51), channel_id=1, source_target_pairs={{32,0},{64,32},{96,64},{128,96},{160,128},{192,160},{224,192},{256... | collective-permute-start | bytes 393224 | tf_op jit(solution)/shard_map/ppermute | solution.py:23
  111.2 3.6 %collective-permute-done = bf16[2,64,1,512]{3,1,2,0:T(8,128)(2,1)S(1)} collective-permute-done((bf16[2,64,1,512]{3,1,2,0:T(8,128)(2,1)S(1)}, bf16[2,64,1,512]{3,1,2,0:T(8,128)(2,1)S(1)}, u32[]{:S(2)}, u32[]{:S(2)}) %collective-permute-start) | collective-permute-done | bytes 131104 | tf_op jit(solution)/shard_map/ppermute | solution.py:23
  115.0 1.5 fusion.1
  117.4 31.5 %shard_map.68 = f32[4,8,32,128]{3,2,1,0:T(8,128)} custom-call(f32[4,8,32,128]{3,2,1,0:T(8,128)} %bitcast.80), custom_call_target="tpu_custom_call" | custom-call | tf_op jit(solution)/shard_map/pallas_call | solution.py:224
  148.9 1.4 copy.44
  150.3 1.2 fusion.27
  151.5 3.5 %fusion = f32[256,8,256]{2,0,1:T(8,128)S(1)} fusion(f32[8,128,128]{2,1,0:T(8,128)S(1)} %get-tuple-element.18, f32[8,128,128]{2,1,0:T(8,128)S(1)} %get-tuple-element.17, f32[8,128,128]{2,1,0:T(8,128)S(1)} %get-tuple-element.16, f32[8,256,256]{2,1,0:T(8,128)S(1)} %copy-done.1), kind=kOutput, calls=%fused_computation.2 | convolution fusion | flops 1613234176 | bytes 5767168 | tf_op jit(solution)/shard_map/krd,kre->kde/dot_general | solution.py:279
  155.0 1.2 copy.60
  156.3 51.2 %shard_map.69 = (f32[2048,256]{1,0:T(8,128)S(1)}, f32[8,256]{1,0:T(8,128)S(1)}) custom-call(f32[2048,256]{1,0:T(8,128)S(1)} %bitcast.70, f32[8,256]{1,0:T(8,128)S(1)} %copy-done), custom_call_target="tpu_custom_call" | custom-call | tf_op jit(solution)/shard_map/pallas_call | solution.py:244
  (45 shorter events, 5.2 us)
Async XLA Ops:
  13.4 39.8 %all-to-all-start = ((bf16[16,2,16384]{2,1,0:T(2,128)(2,1)}), bf16[16,2,16384]{2,1,0:T(2,128)(2,1)S(1)}, u32[]{:S(2)}, u32[]{:S(2)}) async-start(bf16[16,2,16384]{2,1,0:T(2,128)(2,1)} %reshape.130), calls=%async_computation | async-start | bytes 2097152 | tf_op jit(solution)/shard_map/all_to_all | solution.py:262
  25.2 81.2 %all-gather.2.cloned.1.call-start = ((), (), s32[]{:S(2)}) async-start(), calls=%async_computation.2 | async-start | bytes 2162688 | tf_op jit(solution)/shard_map/all_gather | solution.py:260
  63.3 6.1 %copy-start.8 = (s32[8,4]{0,1:T(4,128)S(1)}, s32[8,4]{0,1:T(4,128)}, u32[]{:S(2)}) copy-start(s32[8,4]{0,1:T(4,128)} %param.6) | copy-start | bytes 388
  63.3 6.1 %copy-start.9 = (s32[4]{0:T(128)S(1)}, s32[4]{0:T(128)}, u32[]{:S(2)}) copy-start(s32[4]{0:T(128)} %param.7) | copy-start | bytes 52
  65.6 31.3 %all-to-all-start.1 = ((bf16[16,2,16384]{2,1,0:T(2,128)(2,1)}), bf16[16,2,16384]{2,1,0:T(2,128)(2,1)S(1)}, u32[]{:S(2)}, u32[]{:S(2)}) async-start(bf16[16,2,16384]{2,1,0:T(2,128)(2,1)} %reshape.132), calls=%async_computation.1 | async-start | bytes 2097152 | tf_op jit(solution)/shard_map/all_to_all | solution.py:263
  107.2 7.7 %collective-permute-start = (bf16[2,64,1,512]{3,1,2,0:T(8,128)(2,1)S(1)}, bf16[2,64,1,512]{3,1,2,0:T(8,128)(2,1)S(1)}, u32[]{:S(2)}, u32[]{:S(2)}) collective-permute-start(bf16[2,64,1,512]{3,1,2,0:T(8,128)(2,1)S(1)} %slice.51), channel_id=1, source_target_pairs={{32,0},{64,32},{96,64},{128,96},{160,128},{192,160},{224,192},{256... | collective-permute-start | bytes 393224 | tf_op jit(solution)/shard_map/ppermute | solution.py:23
  111.2 5.3 %copy-start.2 = (bf16[64,8,512]{2,0,1:T(8,128)(2,1)}, bf16[64,8,512]{2,0,1:T(8,128)(2,1)S(1)}, u32[]{:S(2)}) copy-start(bf16[64,8,512]{2,0,1:T(8,128)(2,1)S(1)} %get-tuple-element.20) | copy-start | bytes 1572868
  115.0 1.5 copy-start.4
  115.0 1.5 copy-start.6
  148.9 2.6 %copy-start.1 = (f32[8,256,256]{2,1,0:T(8,128)S(1)}, f32[8,256,256]{2,1,0:T(8,128)}, u32[]{:S(2)}) copy-start(f32[8,256,256]{2,1,0:T(8,128)} %all-gather.2.cloned.1.call-done) | copy-start | bytes 6291460
  155.0 1.3 copy-start
  156.3 51.9 %copy-start.3 = (bf16[64,8,512]{2,0,1:T(8,128)(2,1)S(1)}, bf16[64,8,512]{2,0,1:T(8,128)(2,1)}, u32[]{:S(2)}) copy-start(bf16[64,8,512]{2,0,1:T(8,128)(2,1)} %copy-done.2) | copy-start | bytes 1572868
  156.3 51.9 %copy-start.5 = (bf16[64,8,512]{2,0,1:T(8,128)(2,1)S(1)}, bf16[64,8,512]{2,0,1:T(8,128)(2,1)}, u32[]{:S(2)}) copy-start(bf16[64,8,512]{2,0,1:T(8,128)(2,1)} %copy-done.4) | copy-start | bytes 1572868
  156.3 51.9 %copy-start.7 = (bf16[64,8,512]{2,0,1:T(8,128)(2,1)S(1)}, bf16[64,8,512]{2,0,1:T(8,128)(2,1)}, u32[]{:S(2)}) copy-start(bf16[64,8,512]{2,0,1:T(8,128)(2,1)} %copy-done.6) | copy-start | bytes 1572868
Sparse Core Ops, SparseCore 0:
  29.1 77.2 all-gather.1

commit v4 on v3

--- a/solution.py
+++ b/solution.py
@@ -259,11 +259,10 @@
     rows = prior_factor.shape[1]
     prior = lax.all_gather(prior_factor, "rng", axis=1, tiled=True)
     table = dft_table(cube.shape[2] * lax.axis_size("dop"))
-    pulse_block = lax.all_to_all(cube, "dop", split_axis=3, concat_axis=2, tiled=True)
+    pulse_block = lax.all_to_all(cube, "dop", split_axis=1, concat_axis=2, tiled=True)
     spectrum = lax.all_to_all(
-        spectra(pulse_block, table), "dop", split_axis=2, concat_axis=3, tiled=True
+        spectra(pulse_block, table), "dop", split_axis=2, concat_axis=1, tiled=True
     )
-    spectrum, prior = lax.optimization_barrier((spectrum, prior))
     neighbor = from_behind(spectrum[:, :, 0:1, :], "dop", -1)
     following = jnp.concatenate([spectrum[:, :, 1:, :], neighbor], axis=2)
     vectors = jnp.concatenate([spectrum[0], following[0], spectrum[1], following[1]], axis=0)
@@ -276,10 +275,12 @@
     cross = gram[:, half:, :half] - gram[:, :half, half:]
     row_id = lax.broadcasted_iota(jnp.int32, (1, half, half), 1)
     col_id = lax.broadcasted_iota(jnp.int32, (1, half, half), 2)
+    packed = jnp.where(row_id <= col_id, real_part, cross)
+    packed, prior = lax.optimization_barrier((packed, prior))
     prior_gram = forgetting * jnp.einsum(
         "krd,kre->kde", prior, prior, precision=lax.Precision.HIGHEST
     )
-    packed = sum_over_rng(jnp.where(row_id <= col_id, real_part, cross))
+    packed = sum_over_rng(packed)
     flipped = jnp.swapaxes(packed, 1, 2)
     real_part = jnp.where(row_id <= col_id, packed, flipped)
     cross = jnp.where(row_id > col_id, packed, jnp.where(row_id < col_id, -flipped, 0.0))

time: 218 us -> 203 us (0.931)
  the two profiles are of different devices: /device:TPU:1 before, /device:TPU:4 now
where the time goes in v4:
time: 203 us; the launch traced here: 202 us
  Pallas kernels  81.3 us (40%)
  waiting for transfers between devices  71.7 us (35%)
  starting transfers between devices  16.1 us (8%)
  between operations  14.4 us (7%)
  local copies, waits for them, and re-layouts  9.64 us (5%)
  matrix products  6.36 us (3%)
  other arithmetic  2.9 us (1%)
    pallas_call x1, Pallas kernels, factorize(): pl.pallas_call(factor_kernel, out_shape=(jax.ShapeDtypeStruct((n * BINS,...  51.2 us
    pallas_call x1, Pallas kernels, sum_over_rng(): pl.pallas_call(functools.partial(sum_kernel, nx, ny), out_shape=jax.Shape...  30.1 us
    all_to_all x1, waiting for transfers between devices, shards(): lax.all_to_all(spectra(pulse_block, table), 'dop', split_axis=2, concat_a...  26.3 us
    all_to_all x1, waiting for transfers between devices, shards(): lax.all_to_all(cube, 'dop', split_axis=1, concat_axis=2, tiled=True)  25.2 us
    all_gather x1, waiting for transfers between devices, shards(): prior = lax.all_gather(prior_factor, 'rng', axis=1, tiled=True)  17.8 us
    all_to_all x1, starting transfers between devices, shards(): lax.all_to_all(cube, 'dop', split_axis=1, concat_axis=2, tiled=True)  10.4 us
    all_to_all x1, starting transfers between devices, shards(): lax.all_to_all(spectra(pulse_block, table), 'dop', split_axis=2, concat_a...  4.94 us
  transfers between devices with their start and end apart: 4, of which 4 were waited for; matrix products, arithmetic and copies ran while one was open for 4% of the time, Pallas kernels for 0%

profile of v4, /device:TPU:4, one launch (start us, length us, event | category | flops | bytes accessed | tf_op | source)
XLA Modules:
  0.0 202.4 jit_solution(7520275838460409430)
XLA Ops:
  7.2 2.4 %copy.19 = bf16[2,64,8,512]{3,2,0,1:T(8,128)(2,1)} copy(bf16[2,64,8,512]{3,2,1,0:T(8,128)(2,1)} %param.5) | data formatting | bytes 2097152 | tf_op args[0]
  9.5 10.4 %all-to-all-start = ((bf16[2,64,8,512]{3,2,0,1:T(8,128)(2,1)}), bf16[2,64,8,512]{3,2,0,1:T(8,128)(2,1)S(1)}, u32[]{:S(2)}, u32[]{:S(2)}) async-start(bf16[2,64,8,512]{3,2,0,1:T(8,128)(2,1)} %copy.19), calls=%async_computation | async-start | bytes 2097152 | tf_op jit(solution)/shard_map/all_to_all | solution.py:262
  20.0 0.7 all-gather.2.cloned.1.call-update
  21.3 25.2 %all-to-all-done = bf16[2,64,8,512]{3,2,0,1:T(8,128)(2,1)S(1)} async-done(((bf16[2,64,8,512]{3,2,0,1:T(8,128)(2,1)}), bf16[2,64,8,512]{3,2,0,1:T(8,128)(2,1)S(1)}, u32[]{:S(2)}, u32[]{:S(2)}) %all-to-all-start) | async-done | bytes 1048608 | tf_op jit(solution)/shard_map/all_to_all | solution.py:262
  46.5 1.0 fusion.3
  47.5 1.8 copy.21
  49.3 4.9 %all-to-all-start.1 = ((bf16[2,4,128,512]{3,1,0,2:T(4,128)(2,1)}), bf16[2,4,128,512]{3,1,0,2:T(4,128)(2,1)S(1)}, u32[]{:S(2)}, u32[]{:S(2)}) async-start(bf16[2,4,128,512]{3,1,0,2:T(4,128)(2,1)} %copy.21), calls=%async_computation.1 | async-start | bytes 2097152 | tf_op jit(solution)/shard_map/all_to_all | solution.py:263
  54.5 26.3 %all-to-all-done.1 = bf16[2,4,128,512]{3,1,0,2:T(4,128)(2,1)S(1)} async-done(((bf16[2,4,128,512]{3,1,0,2:T(4,128)(2,1)}), bf16[2,4,128,512]{3,1,0,2:T(4,128)(2,1)S(1)}, u32[]{:S(2)}, u32[]{:S(2)}) %all-to-all-start.1) | async-done | bytes 1048608 | tf_op jit(solution)/shard_map/all_to_all | solution.py:263
  80.7 0.5 copy.43
  81.5 0.7 collective-permute-start
  82.2 0.4 fusion.30
  82.9 1.8 collective-permute-done
  84.9 1.4 fusion.1
  86.3 0.9 fusion.9
  87.2 17.8 %all-gather.2.cloned.1.call-done = f32[8,256,256]{2,1,0:T(8,128)} async-done(((f32[8,8,256]{2,1,0:T(8,128)}), f32[8,256,256]{2,1,0:T(8,128)}) %all-gather.2.cloned.1.call-update) | async-done | bytes 2097168 | tf_op jit(solution)/shard_map/all_gather | solution.py:260
  105.0 30.1 %shard_map.68 = f32[4,8,32,128]{3,2,1,0:T(8,128)} custom-call(f32[4,8,32,128]{3,2,1,0:T(8,128)} %bitcast.77), custom_call_target="tpu_custom_call" | custom-call | tf_op jit(solution)/shard_map/pallas_call | solution.py:224
  135.2 1.4 copy.23
  136.6 1.2 fusion.28
  137.8 3.6 %fusion = f32[256,8,256]{2,0,1:T(8,128)S(1)} fusion(f32[8,128,128]{2,1,0:T(8,128)S(1)} %get-tuple-element.16, f32[8,128,128]{2,1,0:T(8,128)S(1)} %get-tuple-element.15, f32[8,128,128]{2,1,0:T(8,128)S(1)} %get-tuple-element.14, f32[8,256,256]{2,1,0:T(8,128)S(1)} %copy-done.1), kind=kOutput, calls=%fused_computation.2 | convolution fusion | flops 1613234176 | bytes 5767168 | tf_op jit(solution)/shard_map/krd,kre->kde/dot_general | solution.py:280
  141.4 1.2 copy.42
  142.7 51.2 %shard_map.69 = (f32[2048,256]{1,0:T(8,128)S(1)}, f32[8,256]{1,0:T(8,128)S(1)}) custom-call(f32[2048,256]{1,0:T(8,128)S(1)} %bitcast.69, f32[8,256]{1,0:T(8,128)S(1)} %copy-done), custom_call_target="tpu_custom_call" | custom-call | tf_op jit(solution)/shard_map/pallas_call | solution.py:244
  193.9 0.7 copy.44
  194.6 0.4 convolution_bitcast_fusion
  194.9 0.6 copy.28
  (44 shorter events, 1.5 us)
Async XLA Ops:
  9.5 36.9 %all-to-all-start = ((bf16[2,64,8,512]{3,2,0,1:T(8,128)(2,1)}), bf16[2,64,8,512]{3,2,0,1:T(8,128)(2,1)S(1)}, u32[]{:S(2)}, u32[]{:S(2)}) async-start(bf16[2,64,8,512]{3,2,0,1:T(8,128)(2,1)} %copy.19), calls=%async_computation | async-start | bytes 2097152 | tf_op jit(solution)/shard_map/all_to_all | solution.py:262
  20.0 85.1 %all-gather.2.cloned.1.call-start = ((), (), s32[]{:S(2)}) async-start(), calls=%async_computation.2 | async-start | bytes 2162688 | tf_op jit(solution)/shard_map/all_gather | solution.py:260
  47.5 6.8 %copy-start.9 = (s32[8,4]{0,1:T(4,128)S(1)}, s32[8,4]{0,1:T(4,128)}, u32[]{:S(2)}) copy-start(s32[8,4]{0,1:T(4,128)} %param.6) | copy-start | bytes 388
  47.5 6.8 %copy-start.10 = (s32[4]{0:T(128)S(1)}, s32[4]{0:T(128)}, u32[]{:S(2)}) copy-start(s32[4]{0:T(128)} %param.7) | copy-start | bytes 52
  49.3 31.4 %all-to-all-start.1 = ((bf16[2,4,128,512]{3,1,0,2:T(4,128)(2,1)}), bf16[2,4,128,512]{3,1,0,2:T(4,128)(2,1)S(1)}, u32[]{:S(2)}, u32[]{:S(2)}) async-start(bf16[2,4,128,512]{3,1,0,2:T(4,128)(2,1)} %copy.21), calls=%async_computation.1 | async-start | bytes 2097152 | tf_op jit(solution)/shard_map/all_to_all | solution.py:263
  81.5 1.1 copy-start.2
  81.5 3.2 %collective-permute-start = (bf16[2,64,1,512]{3,1,2,0:T(8,128)(2,1)S(1)}, bf16[2,64,1,512]{3,1,2,0:T(8,128)(2,1)S(1)}, u32[]{:S(2)}, u32[]{:S(2)}) collective-permute-start(bf16[2,64,1,512]{3,1,2,0:T(8,128)(2,1)S(1)} %slice.53), channel_id=1, source_target_pairs={{32,0},{64,32},{96,64},{128,96},{160,128},{192,160},{224,192},{256... | collective-permute-start | bytes 393224 | tf_op jit(solution)/shard_map/ppermute | solution.py:23
  82.6 2.1 %slice-start = ((bf16[2,64,8,512]{3,1,2,0:T(8,128)(2,1)}), bf16[2,64,7,512]{3,1,2,0:T(8,128)(2,1)S(1)}, s32[]{:S(2)}) async-start(bf16[2,64,8,512]{3,1,2,0:T(8,128)(2,1)} %copy-done.2), calls=%async_computation.3 | async-start | bytes 1835008 | tf_op jit(solution)/shard_map/slice | solution.py:267
  82.8 3.5 %copy-start.3 = (bf16[64,8,512]{2,0,1:T(8,128)(2,1)}, bf16[64,8,512]{2,0,1:T(8,128)(2,1)S(1)}, u32[]{:S(2)}) copy-start(bf16[64,8,512]{2,0,1:T(8,128)(2,1)S(1)} %squeeze.12) | copy-start | bytes 1572868
  84.9 1.5 copy-start.5
  84.9 1.5 copy-start.7
  135.2 2.6 %copy-start.1 = (f32[8,256,256]{2,1,0:T(8,128)S(1)}, f32[8,256,256]{2,1,0:T(8,128)}, u32[]{:S(2)}) copy-start(f32[8,256,256]{2,1,0:T(8,128)} %all-gather.2.cloned.1.call-done) | copy-start | bytes 6291460
  141.4 1.3 copy-start
  142.6 51.9 %copy-start.4 = (bf16[64,8,512]{2,0,1:T(8,128)(2,1)S(1)}, bf16[64,8,512]{2,0,1:T(8,128)(2,1)}, u32[]{:S(2)}) copy-start(bf16[64,8,512]{2,0,1:T(8,128)(2,1)} %copy-done.3) | copy-start | bytes 1572868
  142.6 51.9 %copy-start.6 = (bf16[64,8,512]{2,0,1:T(8,128)(2,1)S(1)}, bf16[64,8,512]{2,0,1:T(8,128)(2,1)}, u32[]{:S(2)}) copy-start(bf16[64,8,512]{2,0,1:T(8,128)(2,1)} %copy-done.5) | copy-start | bytes 1572868
  142.6 51.9 %copy-start.8 = (bf16[64,8,512]{2,0,1:T(8,128)(2,1)S(1)}, bf16[64,8,512]{2,0,1:T(8,128)(2,1)}, u32[]{:S(2)}) copy-start(bf16[64,8,512]{2,0,1:T(8,128)(2,1)} %copy-done.7) | copy-start | bytes 1572868
Sparse Core Ops, SparseCore 0:
  23.8 81.1 all-gather.1

commit v5 on v4

--- a/solution.py
+++ b/solution.py
@@ -275,12 +275,11 @@
     cross = gram[:, half:, :half] - gram[:, :half, half:]
     row_id = lax.broadcasted_iota(jnp.int32, (1, half, half), 1)
     col_id = lax.broadcasted_iota(jnp.int32, (1, half, half), 2)
-    packed = jnp.where(row_id <= col_id, real_part, cross)
+    packed = sum_over_rng(jnp.where(row_id <= col_id, real_part, cross))
     packed, prior = lax.optimization_barrier((packed, prior))
     prior_gram = forgetting * jnp.einsum(
         "krd,kre->kde", prior, prior, precision=lax.Precision.HIGHEST
     )
-    packed = sum_over_rng(packed)
     flipped = jnp.swapaxes(packed, 1, 2)
     real_part = jnp.where(row_id <= col_id, packed, flipped)
     cross = jnp.where(row_id > col_id, packed, jnp.where(row_id < col_id, -flipped, 0.0))

time: 203 us -> 194 us (0.956)
  the two profiles are of different devices: /device:TPU:4 before, /device:TPU:1 now
where the time goes in v5:
time: 194 us
  Pallas kernels  86 us (44%)
  waiting for transfers between devices  58.3 us (30%)
  starting transfers between devices  15.6 us (8%)
  between operations  14.4 us (7%)
  local copies, waits for them, and re-layouts  10.2 us (5%)
  matrix products  6.36 us (3%)
  other arithmetic  2.9 us (1%)
    pallas_call x1, Pallas kernels, factorize(): pl.pallas_call(factor_kernel, out_shape=(jax.ShapeDtypeStruct((n * BINS,...  51.2 us
    pallas_call x1, Pallas kernels, sum_over_rng(): pl.pallas_call(functools.partial(sum_kernel, nx, ny), out_shape=jax.Shape...  34.8 us
    all_to_all x1, waiting for transfers between devices, shards(): lax.all_to_all(spectra(pulse_block, table), 'dop', split_axis=2, concat_a...  27.4 us
    all_to_all x1, waiting for transfers between devices, shards(): lax.all_to_all(cube, 'dop', split_axis=1, concat_axis=2, tiled=True)  26.7 us
    all_to_all x1, starting transfers between devices, shards(): lax.all_to_all(cube, 'dop', split_axis=1, concat_axis=2, tiled=True)  11.8 us
    unnamed x25, local copies, waits for them, and re-layouts  4.26 us
  transfers between devices with their start and end apart: 4, of which 3 were waited for; matrix products, arithmetic and copies ran while one was open for 4% of the time, Pallas kernels for 18%

profile of v5, /device:TPU:1, one launch (start us, length us, event | category | flops | bytes accessed | tf_op | source)
XLA Modules:
  0.0 193.8 jit_solution(5565777780792442707)
XLA Ops:
  7.2 2.4 %copy.19 = bf16[2,64,8,512]{3,2,0,1:T(8,128)(2,1)} copy(bf16[2,64,8,512]{3,2,1,0:T(8,128)(2,1)} %param.5) | data formatting | bytes 2097152 | tf_op args[0]
  9.5 11.8 %all-to-all-start = ((bf16[2,64,8,512]{3,2,0,1:T(8,128)(2,1)}), bf16[2,64,8,512]{3,2,0,1:T(8,128)(2,1)S(1)}, u32[]{:S(2)}, u32[]{:S(2)}) async-start(bf16[2,64,8,512]{3,2,0,1:T(8,128)(2,1)} %copy.19), calls=%async_computation | async-start | bytes 2097152 | tf_op jit(solution)/shard_map/all_to_all | solution.py:262
  21.4 0.7 all-gather.2.cloned.1.call-update
  22.7 26.7 %all-to-all-done = bf16[2,64,8,512]{3,2,0,1:T(8,128)(2,1)S(1)} async-done(((bf16[2,64,8,512]{3,2,0,1:T(8,128)(2,1)}), bf16[2,64,8,512]{3,2,0,1:T(8,128)(2,1)S(1)}, u32[]{:S(2)}, u32[]{:S(2)}) %all-to-all-start) | async-done | bytes 1048608 | tf_op jit(solution)/shard_map/all_to_all | solution.py:262
  49.3 1.0 fusion.3
  50.4 1.8 copy.21
  52.2 3.7 %all-to-all-start.1 = ((bf16[2,4,128,512]{3,1,0,2:T(4,128)(2,1)}), bf16[2,4,128,512]{3,1,0,2:T(4,128)(2,1)S(1)}, u32[]{:S(2)}, u32[]{:S(2)}) async-start(bf16[2,4,128,512]{3,1,0,2:T(4,128)(2,1)} %copy.21), calls=%async_computation.1 | async-start | bytes 2097152 | tf_op jit(solution)/shard_map/all_to_all | solution.py:263
  56.1 27.4 %all-to-all-done.1 = bf16[2,4,128,512]{3,1,0,2:T(4,128)(2,1)S(1)} async-done(((bf16[2,4,128,512]{3,1,0,2:T(4,128)(2,1)}), bf16[2,4,128,512]{3,1,0,2:T(4,128)(2,1)S(1)}, u32[]{:S(2)}, u32[]{:S(2)}) %all-to-all-start.1) | async-done | bytes 1048608 | tf_op jit(solution)/shard_map/all_to_all | solution.py:263
  83.5 0.5 copy.43
  84.0 0.3 all_to_all.33
  84.4 0.4 fusion.30
  84.8 0.5 copy-done.2
  85.6 3.6 %collective-permute-done = bf16[2,64,1,512]{3,1,2,0:T(8,128)(2,1)S(1)} collective-permute-done((bf16[2,64,1,512]{3,1,2,0:T(8,128)(2,1)S(1)}, bf16[2,64,1,512]{3,1,2,0:T(8,128)(2,1)S(1)}, u32[]{:S(2)}, u32[]{:S(2)}) %collective-permute-start) | collective-permute-done | bytes 131104 | tf_op jit(solution)/shard_map/ppermute | solution.py:23
  89.3 1.4 fusion.1
  90.8 0.9 fusion.9
  91.6 34.8 %shard_map.68 = f32[4,8,32,128]{3,2,1,0:T(8,128)} custom-call(f32[4,8,32,128]{3,2,1,0:T(8,128)} %bitcast.77), custom_call_target="tpu_custom_call" | custom-call | tf_op jit(solution)/shard_map/pallas_call | solution.py:224
  126.5 1.4 copy.23
  127.9 1.2 fusion.28
  129.2 3.6 %fusion = f32[256,8,256]{2,0,1:T(8,128)S(1)} fusion(f32[8,128,128]{2,1,0:T(8,128)S(1)} %get-tuple-element.16, f32[8,128,128]{2,1,0:T(8,128)S(1)} %get-tuple-element.15, f32[8,128,128]{2,1,0:T(8,128)S(1)} %get-tuple-element.14, f32[8,256,256]{2,1,0:T(8,128)S(1)} %copy-done.1), kind=kOutput, calls=%fused_computation.2 | convolution fusion | flops 1613234176 | bytes 5767168 | tf_op jit(solution)/shard_map/krd,kre->kde/dot_general | solution.py:280
  132.7 1.2 copy.42
  134.0 51.2 %shard_map.69 = (f32[2048,256]{1,0:T(8,128)S(1)}, f32[8,256]{1,0:T(8,128)S(1)}) custom-call(f32[2048,256]{1,0:T(8,128)S(1)} %bitcast.69, f32[8,256]{1,0:T(8,128)S(1)} %copy-done), custom_call_target="tpu_custom_call" | custom-call | tf_op jit(solution)/shard_map/pallas_call | solution.py:244
  185.2 0.7 copy.44
  185.9 0.4 convolution_bitcast_fusion
  186.3 0.6 copy.28
  (44 shorter events, 1.3 us)
Async XLA Ops:
  9.5 39.8 %all-to-all-start = ((bf16[2,64,8,512]{3,2,0,1:T(8,128)(2,1)}), bf16[2,64,8,512]{3,2,0,1:T(8,128)(2,1)S(1)}, u32[]{:S(2)}, u32[]{:S(2)}) async-start(bf16[2,64,8,512]{3,2,0,1:T(8,128)(2,1)} %copy.19), calls=%async_computation | async-start | bytes 2097152 | tf_op jit(solution)/shard_map/all_to_all | solution.py:262
  21.4 105.1 %all-gather.2.cloned.1.call-start = ((), (), s32[]{:S(2)}) async-start(), calls=%async_computation.2 | async-start | bytes 2162688 | tf_op jit(solution)/shard_map/all_gather | solution.py:260
  50.3 5.6 %copy-start.9 = (s32[8,4]{0,1:T(4,128)S(1)}, s32[8,4]{0,1:T(4,128)}, u32[]{:S(2)}) copy-start(s32[8,4]{0,1:T(4,128)} %param.6) | copy-start | bytes 388
  50.4 5.6 %copy-start.10 = (s32[4]{0:T(128)S(1)}, s32[4]{0:T(128)}, u32[]{:S(2)}) copy-start(s32[4]{0:T(128)} %param.7) | copy-start | bytes 52
  52.2 31.4 %all-to-all-start.1 = ((bf16[2,4,128,512]{3,1,0,2:T(4,128)(2,1)}), bf16[2,4,128,512]{3,1,0,2:T(4,128)(2,1)S(1)}, u32[]{:S(2)}, u32[]{:S(2)}) async-start(bf16[2,4,128,512]{3,1,0,2:T(4,128)(2,1)} %copy.21), calls=%async_computation.1 | async-start | bytes 2097152 | tf_op jit(solution)/shard_map/all_to_all | solution.py:263
  84.3 1.0 copy-start.2
  84.3 4.8 %collective-permute-start = (bf16[2,64,1,512]{3,1,2,0:T(8,128)(2,1)S(1)}, bf16[2,64,1,512]{3,1,2,0:T(8,128)(2,1)S(1)}, u32[]{:S(2)}, u32[]{:S(2)}) collective-permute-start(bf16[2,64,1,512]{3,1,2,0:T(8,128)(2,1)S(1)} %slice.53), channel_id=1, source_target_pairs={{32,0},{64,32},{96,64},{128,96},{160,128},{192,160},{224,192},{256... | collective-permute-start | bytes 393224 | tf_op jit(solution)/shard_map/ppermute | solution.py:23
  85.3 3.8 %slice-start = ((bf16[2,64,8,512]{3,1,2,0:T(8,128)(2,1)}), bf16[2,64,7,512]{3,1,2,0:T(8,128)(2,1)S(1)}, s32[]{:S(2)}) async-start(bf16[2,64,8,512]{3,1,2,0:T(8,128)(2,1)} %copy-done.2), calls=%async_computation.3 | async-start | bytes 1835008 | tf_op jit(solution)/shard_map/slice | solution.py:267
  85.4 5.3 %copy-start.3 = (bf16[64,8,512]{2,0,1:T(8,128)(2,1)}, bf16[64,8,512]{2,0,1:T(8,128)(2,1)S(1)}, u32[]{:S(2)}) copy-start(bf16[64,8,512]{2,0,1:T(8,128)(2,1)S(1)} %squeeze.12) | copy-start | bytes 1572868
  89.3 1.5 copy-start.5
  89.3 1.5 copy-start.7
  126.5 2.6 %copy-start.1 = (f32[8,256,256]{2,1,0:T(8,128)S(1)}, f32[8,256,256]{2,1,0:T(8,128)}, u32[]{:S(2)}) copy-start(f32[8,256,256]{2,1,0:T(8,128)} %all-gather.2.cloned.1.call-done) | copy-start | bytes 6291460
  132.7 1.3 copy-start
  134.0 51.9 %copy-start.4 = (bf16[64,8,512]{2,0,1:T(8,128)(2,1)S(1)}, bf16[64,8,512]{2,0,1:T(8,128)(2,1)}, u32[]{:S(2)}) copy-start(bf16[64,8,512]{2,0,1:T(8,128)(2,1)} %copy-done.3) | copy-start | bytes 1572868
  134.0 51.9 %copy-start.6 = (bf16[64,8,512]{2,0,1:T(8,128)(2,1)S(1)}, bf16[64,8,512]{2,0,1:T(8,128)(2,1)}, u32[]{:S(2)}) copy-start(bf16[64,8,512]{2,0,1:T(8,128)(2,1)} %copy-done.5) | copy-start | bytes 1572868
  134.0 51.9 %copy-start.8 = (bf16[64,8,512]{2,0,1:T(8,128)(2,1)S(1)}, bf16[64,8,512]{2,0,1:T(8,128)(2,1)}, u32[]{:S(2)}) copy-start(bf16[64,8,512]{2,0,1:T(8,128)(2,1)} %copy-done.7) | copy-start | bytes 1572868
Sparse Core Ops, SparseCore 0:
  25.2 76.9 all-gather.1

commit v6 on v5

--- a/solution.py
+++ b/solution.py
@@ -125,13 +125,14 @@
         bottom = pl.ds(LANES * BINS + b, LANES, stride=BINS)
         upper = right[top, :]
         inverse = jnp.where(col_id <= row_id, left[top, :], 0.0)
-        across = upper.T
-        left[bottom, :] = -jnp.dot(
-            across, inverse, precision=lax.Precision.HIGHEST, preferred_element_type=jnp.float32
+        both = jnp.dot(
+            upper.T,
+            jnp.concatenate([inverse, upper], axis=1),
+            precision=lax.Precision.HIGHEST,
+            preferred_element_type=jnp.float32,
         )
-        right[bottom, :] = right[bottom, :] - jnp.dot(
-            across, upper, precision=lax.Precision.HIGHEST, preferred_element_type=jnp.float32
-        )
+        left[bottom, :] = -both[:, :LANES]
+        right[bottom, :] = right[bottom, :] - both[:, LANES:]
 
     s, q, vv = lax.fori_loop(0, LANES // PANEL, lambda p, c: panel(1, p, c), carry)
     for c in range(2):

time: 194 us -> 194 us (level)
  no operation moved by 1% of the time
where the time goes in v6:
time: 194 us
  Pallas kernels  85.8 us (44%)
  waiting for transfers between devices  58.3 us (30%)
  starting transfers between devices  15.6 us (8%)
  between operations  14.4 us (7%)
  local copies, waits for them, and re-layouts  10.2 us (5%)
  matrix products  6.36 us (3%)
  other arithmetic  2.9 us (1%)
    pallas_call x1, Pallas kernels, factorize(): pl.pallas_call(factor_kernel, out_shape=(jax.ShapeDtypeStruct((n * BINS,...  51 us
    pallas_call x1, Pallas kernels, sum_over_rng(): pl.pallas_call(functools.partial(sum_kernel, nx, ny), out_shape=jax.Shape...  34.8 us
    all_to_all x1, waiting for transfers between devices, shards(): lax.all_to_all(spectra(pulse_block, table), 'dop', split_axis=2, concat_a...  27.4 us
    all_to_all x1, waiting for transfers between devices, shards(): lax.all_to_all(cube, 'dop', split_axis=1, concat_axis=2, tiled=True)  26.7 us
    all_to_all x1, starting transfers between devices, shards(): lax.all_to_all(cube, 'dop', split_axis=1, concat_axis=2, tiled=True)  11.8 us
    unnamed x25, local copies, waits for them, and re-layouts  4.26 us
  transfers between devices with their start and end apart: 4, of which 3 were waited for; matrix products, arithmetic and copies ran while one was open for 4% of the time, Pallas kernels for 18%

profile of v6, /device:TPU:1, one launch (start us, length us, event | category | flops | bytes accessed | tf_op | source)
XLA Modules:
  0.0 193.6 jit_solution(8707009990242559983)
XLA Ops:
  7.2 2.4 %copy.19 = bf16[2,64,8,512]{3,2,0,1:T(8,128)(2,1)} copy(bf16[2,64,8,512]{3,2,1,0:T(8,128)(2,1)} %param.5) | data formatting | bytes 2097152 | tf_op args[0]
  9.5 11.8 %all-to-all-start = ((bf16[2,64,8,512]{3,2,0,1:T(8,128)(2,1)}), bf16[2,64,8,512]{3,2,0,1:T(8,128)(2,1)S(1)}, u32[]{:S(2)}, u32[]{:S(2)}) async-start(bf16[2,64,8,512]{3,2,0,1:T(8,128)(2,1)} %copy.19), calls=%async_computation | async-start | bytes 2097152 | tf_op jit(solution)/shard_map/all_to_all | solution.py:263
  21.4 0.7 all-gather.2.cloned.1.call-update
  22.7 26.7 %all-to-all-done = bf16[2,64,8,512]{3,2,0,1:T(8,128)(2,1)S(1)} async-done(((bf16[2,64,8,512]{3,2,0,1:T(8,128)(2,1)}), bf16[2,64,8,512]{3,2,0,1:T(8,128)(2,1)S(1)}, u32[]{:S(2)}, u32[]{:S(2)}) %all-to-all-start) | async-done | bytes 1048608 | tf_op jit(solution)/shard_map/all_to_all | solution.py:263
  49.3 1.0 fusion.3
  50.4 1.8 copy.21
  52.2 3.7 %all-to-all-start.1 = ((bf16[2,4,128,512]{3,1,0,2:T(4,128)(2,1)}), bf16[2,4,128,512]{3,1,0,2:T(4,128)(2,1)S(1)}, u32[]{:S(2)}, u32[]{:S(2)}) async-start(bf16[2,4,128,512]{3,1,0,2:T(4,128)(2,1)} %copy.21), calls=%async_computation.1 | async-start | bytes 2097152 | tf_op jit(solution)/shard_map/all_to_all | solution.py:264
  56.1 27.4 %all-to-all-done.1 = bf16[2,4,128,512]{3,1,0,2:T(4,128)(2,1)S(1)} async-done(((bf16[2,4,128,512]{3,1,0,2:T(4,128)(2,1)}), bf16[2,4,128,512]{3,1,0,2:T(4,128)(2,1)S(1)}, u32[]{:S(2)}, u32[]{:S(2)}) %all-to-all-start.1) | async-done | bytes 1048608 | tf_op jit(solution)/shard_map/all_to_all | solution.py:264
  83.5 0.5 copy.43
  84.0 0.3 all_to_all.33
  84.4 0.4 fusion.30
  84.8 0.5 copy-done.2
  85.6 3.6 %collective-permute-done = bf16[2,64,1,512]{3,1,2,0:T(8,128)(2,1)S(1)} collective-permute-done((bf16[2,64,1,512]{3,1,2,0:T(8,128)(2,1)S(1)}, bf16[2,64,1,512]{3,1,2,0:T(8,128)(2,1)S(1)}, u32[]{:S(2)}, u32[]{:S(2)}) %collective-permute-start) | collective-permute-done | bytes 131104 | tf_op jit(solution)/shard_map/ppermute | solution.py:23
  89.3 1.4 fusion.1
  90.8 0.9 fusion.9
  91.6 34.8 %shard_map.68 = f32[4,8,32,128]{3,2,1,0:T(8,128)} custom-call(f32[4,8,32,128]{3,2,1,0:T(8,128)} %bitcast.77), custom_call_target="tpu_custom_call" | custom-call | tf_op jit(solution)/shard_map/pallas_call | solution.py:225
  126.5 1.4 copy.23
  127.9 1.2 fusion.28
  129.2 3.6 %fusion = f32[256,8,256]{2,0,1:T(8,128)S(1)} fusion(f32[8,128,128]{2,1,0:T(8,128)S(1)} %get-tuple-element.16, f32[8,128,128]{2,1,0:T(8,128)S(1)} %get-tuple-element.15, f32[8,128,128]{2,1,0:T(8,128)S(1)} %get-tuple-element.14, f32[8,256,256]{2,1,0:T(8,128)S(1)} %copy-done.1), kind=kOutput, calls=%fused_computation.2 | convolution fusion | flops 1613234176 | bytes 5767168 | tf_op jit(solution)/shard_map/krd,kre->kde/dot_general | solution.py:281
  132.7 1.2 copy.42
  134.0 51.0 %shard_map.69 = (f32[2048,256]{1,0:T(8,128)S(1)}, f32[8,256]{1,0:T(8,128)S(1)}) custom-call(f32[2048,256]{1,0:T(8,128)S(1)} %bitcast.69, f32[8,256]{1,0:T(8,128)S(1)} %copy-done), custom_call_target="tpu_custom_call" | custom-call | tf_op jit(solution)/shard_map/pallas_call | solution.py:245
  185.1 0.7 copy.44
  185.8 0.4 convolution_bitcast_fusion
  186.1 0.6 copy.28
  (44 shorter events, 1.3 us)
Async XLA Ops:
  9.5 39.8 %all-to-all-start = ((bf16[2,64,8,512]{3,2,0,1:T(8,128)(2,1)}), bf16[2,64,8,512]{3,2,0,1:T(8,128)(2,1)S(1)}, u32[]{:S(2)}, u32[]{:S(2)}) async-start(bf16[2,64,8,512]{3,2,0,1:T(8,128)(2,1)} %copy.19), calls=%async_computation | async-start | bytes 2097152 | tf_op jit(solution)/shard_map/all_to_all | solution.py:263
  21.4 105.1 %all-gather.2.cloned.1.call-start = ((), (), s32[]{:S(2)}) async-start(), calls=%async_computation.2 | async-start | bytes 2162688 | tf_op jit(solution)/shard_map/all_gather | solution.py:261
  50.3 5.6 %copy-start.9 = (s32[8,4]{0,1:T(4,128)S(1)}, s32[8,4]{0,1:T(4,128)}, u32[]{:S(2)}) copy-start(s32[8,4]{0,1:T(4,128)} %param.6) | copy-start | bytes 388
  50.4 5.6 %copy-start.10 = (s32[4]{0:T(128)S(1)}, s32[4]{0:T(128)}, u32[]{:S(2)}) copy-start(s32[4]{0:T(128)} %param.7) | copy-start | bytes 52
  52.2 31.4 %all-to-all-start.1 = ((bf16[2,4,128,512]{3,1,0,2:T(4,128)(2,1)}), bf16[2,4,128,512]{3,1,0,2:T(4,128)(2,1)S(1)}, u32[]{:S(2)}, u32[]{:S(2)}) async-start(bf16[2,4,128,512]{3,1,0,2:T(4,128)(2,1)} %copy.21), calls=%async_computation.1 | async-start | bytes 2097152 | tf_op jit(solution)/shard_map/all_to_all | solution.py:264
  84.3 1.0 copy-start.2
  84.3 4.8 %collective-permute-start = (bf16[2,64,1,512]{3,1,2,0:T(8,128)(2,1)S(1)}, bf16[2,64,1,512]{3,1,2,0:T(8,128)(2,1)S(1)}, u32[]{:S(2)}, u32[]{:S(2)}) collective-permute-start(bf16[2,64,1,512]{3,1,2,0:T(8,128)(2,1)S(1)} %slice.53), channel_id=1, source_target_pairs={{32,0},{64,32},{96,64},{128,96},{160,128},{192,160},{224,192},{256... | collective-permute-start | bytes 393224 | tf_op jit(solution)/shard_map/ppermute | solution.py:23
  85.3 3.8 %slice-start = ((bf16[2,64,8,512]{3,1,2,0:T(8,128)(2,1)}), bf16[2,64,7,512]{3,1,2,0:T(8,128)(2,1)S(1)}, s32[]{:S(2)}) async-start(bf16[2,64,8,512]{3,1,2,0:T(8,128)(2,1)} %copy-done.2), calls=%async_computation.3 | async-start | bytes 1835008 | tf_op jit(solution)/shard_map/slice | solution.py:268
  85.4 5.3 %copy-start.3 = (bf16[64,8,512]{2,0,1:T(8,128)(2,1)}, bf16[64,8,512]{2,0,1:T(8,128)(2,1)S(1)}, u32[]{:S(2)}) copy-start(bf16[64,8,512]{2,0,1:T(8,128)(2,1)S(1)} %squeeze.12) | copy-start | bytes 1572868
  89.3 1.5 copy-start.5
  89.3 1.5 copy-start.7
  126.5 2.6 %copy-start.1 = (f32[8,256,256]{2,1,0:T(8,128)S(1)}, f32[8,256,256]{2,1,0:T(8,128)}, u32[]{:S(2)}) copy-start(f32[8,256,256]{2,1,0:T(8,128)} %all-gather.2.cloned.1.call-done) | copy-start | bytes 6291460
  132.7 1.3 copy-start
  134.0 51.8 %copy-start.4 = (bf16[64,8,512]{2,0,1:T(8,128)(2,1)S(1)}, bf16[64,8,512]{2,0,1:T(8,128)(2,1)}, u32[]{:S(2)}) copy-start(bf16[64,8,512]{2,0,1:T(8,128)(2,1)} %copy-done.3) | copy-start | bytes 1572868
  134.0 51.8 %copy-start.6 = (bf16[64,8,512]{2,0,1:T(8,128)(2,1)S(1)}, bf16[64,8,512]{2,0,1:T(8,128)(2,1)}, u32[]{:S(2)}) copy-start(bf16[64,8,512]{2,0,1:T(8,128)(2,1)} %copy-done.5) | copy-start | bytes 1572868
  134.0 51.8 %copy-start.8 = (bf16[64,8,512]{2,0,1:T(8,128)(2,1)S(1)}, bf16[64,8,512]{2,0,1:T(8,128)(2,1)}, u32[]{:S(2)}) copy-start(bf16[64,8,512]{2,0,1:T(8,128)(2,1)} %copy-done.7) | copy-start | bytes 1572868
Sparse Core Ops, SparseCore 0:
  25.2 76.9 all-gather.1
